TPU v7x, 256 devices: a whole 4x4x8 slice. The times are simulated.
256 devices in a mesh: req: 32 (over x, z_hi, core), ctx: 8 (over z_lo, y).
Axes of the slice: x: 4, y: 4, z: 8 (z_hi: 4, z_lo: 2; z = z_hi * 2 + z_lo), core: 2. Of those that a mesh axis runs over, the one named last changes fastest.
Arguments:
- q_heads: bfloat16 [32, 1024, 12288], P('req', 'ctx'), may hold values from -204 to 204
- kv_latent: bfloat16 [32, 1024, 576], P('req', 'ctx'), may hold values from -600 to 600
- latent_gain: float32 [512], replicated, may hold values from 0.1 to 1.9
- kv_up: bfloat16 [64, 256, 512], P('ctx'), may hold values from -0.25 to 0.25
- offsets: int32 [32], P('req'), may hold values from 0 to 7168, as said below
- lengths: int32 [32], P('req'), may hold values from 64 to 1024
- block_order: int32 [32, 16], P('req'), may hold values from 0 to 15, each once within a row
- owners: int32 [32, 16], P(None, 'ctx'), may hold values from 0 to 31, as said below
Outputs:
- attn_out: bfloat16 [32, 1024, 8192], P('req', 'ctx')
- shipped: bfloat16 [32, 16, 36864], P('req', 'ctx')
Inputs may be any that keep to these rules, and one draw needn't show every extreme that they name: `offsets`: each entry is a multiple of 1024. `block_order`: each row names every block index once. `owners`: for each context index j, column 2 j and column 2 j + 1 each name every owner once, and no row names the same owner in both of them.
All inputs are finite; a program needn't handle non-finite values.
Results may differ from a plain program's by a relative error of at most 0.007.
Values may be sent and summed in bfloat16 or wider, within the bound.
No kernel may reach another device: no remote copies, remote signals or barrier semaphores. Data moves between devices by JAX's collectives and lax.ppermute only.
A program may use at most 64 MiB of HBM per device.

v0:
```python
import math

import jax
import jax.numpy as jnp
from jax import lax
from jax.sharding import PartitionSpec as P

HEADS = 64
HD = 128
ROPE = 64
LAT = 512


theta_base = 10000.0
epsilon = 1e-06
masked_fill = -1e30


def as_sent(array):
    return jax.tree.map(lambda a: a.astype(jnp.bfloat16) if a.dtype == jnp.float32 else a, array)


def rotate(values, angles):
    half_width = values.shape[-1] // 2
    first_half = values[..., :half_width]
    second_half = values[..., half_width:]
    cosine = jnp.cos(angles)
    sine_part = jnp.sin(angles)
    return jnp.concatenate(
        [
            first_half * cosine - second_half * sine_part,
            second_half * cosine + first_half * sine_part,
        ],
        axis=-1,
    )


def angle_table(positions, rope_width):
    half_width = rope_width // 2
    frequency = jnp.exp(
        -math.log(theta_base) * jnp.arange(half_width, dtype=jnp.float32) / half_width
    )
    return positions.astype(jnp.float32)[:, None] * frequency[None, :]


def make_cache(latent_rows, latent_gain, angles):
    latent = latent_rows[:, :LAT].astype(jnp.float32)
    mean_square = jnp.mean(latent * latent, axis=-1, keepdims=True)
    normed = (latent * lax.rsqrt(mean_square + epsilon) * latent_gain).astype(jnp.bfloat16)
    key_rope = rotate(latent_rows[:, LAT:].astype(jnp.float32), angles).astype(jnp.bfloat16)
    return jnp.concatenate([normed, key_rope], axis=-1)


def attend(queries, key_rows, value_weight, allowed, valid_rows):
    score_scale = (HD + ROPE) ** (-0.5)
    scores = (
        jnp.einsum("qc,kc->qk", queries, key_rows, preferred_element_type=jnp.float32) * score_scale
    )
    masked = jnp.where(allowed, scores, masked_fill)
    row_max = jnp.max(masked, axis=-1, keepdims=True)
    exponent = jnp.exp(masked - row_max)
    probabilities = (exponent / jnp.sum(exponent, axis=-1, keepdims=True)).astype(jnp.bfloat16)
    output_latent = jnp.dot(
        probabilities, key_rows[:, :LAT], preferred_element_type=jnp.float32
    ).astype(jnp.bfloat16)
    projected = jnp.einsum(
        "qc,dc->qd", output_latent, value_weight, preferred_element_type=jnp.float32
    )
    return jnp.where(valid_rows[:, None], projected, 0.0).astype(jnp.bfloat16)


def latent_query(head_queries, weight):
    query_latent = jnp.dot(
        head_queries[:, :HD], weight[:HD], preferred_element_type=jnp.float32
    ).astype(jnp.bfloat16)
    return jnp.concatenate([query_latent, head_queries[:, HD:]], axis=-1)


def per_device(q_heads, kv_latent, latent_gain, kv_up, offsets, lengths, block_order, owners):
    groups = lax.axis_size("ctx")
    context = lax.axis_index("ctx")
    local_rows = q_heads.shape[1]
    block_width = local_rows // 2
    segment_length = local_rows * groups
    heads_here = kv_up.shape[0]
    order_row = block_order[0]
    length_here = lengths[0]
    row_index = jnp.arange(local_rows, dtype=jnp.int32)
    blocks_here = lax.dynamic_slice_in_dim(order_row, 2 * context, 2)
    positions = blocks_here[row_index // block_width] * block_width + row_index % block_width
    angles = angle_table(offsets[0] + positions, ROPE)
    cache_rows = make_cache(kv_latent[0], latent_gain, angles)
    key_rows = lax.all_gather(cache_rows, "ctx", axis=0, tiled=True)
    query_parts = q_heads[0].reshape(local_rows, HEADS, HD + ROPE)
    query_rope = rotate(query_parts[:, :, HD:].astype(jnp.float32), angles[:, None, :]).astype(
        jnp.bfloat16
    )
    joined = jnp.concatenate([query_parts[:, :, :HD], query_rope], axis=-1)
    outgoing = joined.reshape(local_rows, groups, heads_here * (HD + ROPE))
    incoming = lax.all_to_all(outgoing, "ctx", split_axis=1, concat_axis=0, tiled=True)
    block_ids = jnp.arange(2 * groups, dtype=jnp.int32)
    inverse = jnp.sum(
        jnp.where(order_row[None, :] == block_ids[:, None], block_ids[None, :], 0), axis=1
    )
    sorted_queries = jnp.take(
        incoming.reshape(2 * groups, block_width, heads_here, HD + ROPE), inverse, axis=0
    )
    sorted_queries = sorted_queries.reshape(segment_length, heads_here, HD + ROPE)
    sorted_keys = jnp.take(
        key_rows.reshape(2 * groups, block_width, key_rows.shape[1]), inverse, axis=0
    )
    sorted_keys = sorted_keys.reshape(segment_length, key_rows.shape[1])
    sorted_positions = jnp.arange(segment_length, dtype=jnp.int32)
    tile_rows = min(256, segment_length)

    def one_head(head_index):
        weight = kv_up[head_index]
        head_queries = lax.dynamic_index_in_dim(sorted_queries, head_index, 1, keepdims=False)
        queries = latent_query(head_queries, weight)
        pieces = []
        for tile_index in range(segment_length // tile_rows):
            lower_row = tile_index * tile_rows
            upper_row = lower_row + tile_rows
            query_pos = sorted_positions[lower_row:upper_row]
            key_pos = sorted_positions[:upper_row]
            allowed = (key_pos[None, :] <= query_pos[:, None]) & (key_pos[None, :] < length_here)
            pieces.append(
                attend(
                    queries[lower_row:upper_row],
                    sorted_keys[:upper_row],
                    weight[HD:],
                    allowed,
                    query_pos < length_here,
                )
            )
        return jnp.concatenate(pieces, axis=0)

    per_head = lax.map(one_head, jnp.arange(heads_here, dtype=jnp.int32))
    merged = per_head.transpose(1, 0, 2).reshape(2 * groups, block_width, heads_here * HD)
    device_order = jnp.take(merged, order_row, axis=0).reshape(segment_length, 1, heads_here * HD)
    returned = lax.all_to_all(
        as_sent(device_order), "ctx", split_axis=0, concat_axis=1, tiled=True
    ).astype(device_order.dtype)
    attn_out = returned.reshape(1, local_rows, HEADS * HD)
    page_rows = cache_rows.reshape(2, block_width * cache_rows.shape[1])
    owner_here = lax.axis_index("req")
    everyone = lax.all_gather(page_rows, "req", axis=0, tiled=True)
    named_owner = owners.reshape(-1)
    source_index = jnp.arange(named_owner.shape[0], dtype=jnp.int32)
    matches = named_owner == owner_here
    first_slot = jnp.min(jnp.where(matches, source_index, named_owner.shape[0]))
    second_slot = jnp.min(
        jnp.where(matches & (source_index != first_slot), source_index, named_owner.shape[0])
    )
    picked = jnp.take(everyone, jnp.stack([first_slot, second_slot]), axis=0)
    shipped = picked.reshape(1, 2, page_rows.shape[1])
    return (attn_out, shipped)


def solution(mesh):
    in_specs = (
        P("req", "ctx", None),
        P("req", "ctx", None),
        P(),
        P("ctx", None, None),
        P("req"),
        P("req"),
        P("req", None),
        P(None, "ctx"),
    )
    out_specs = (P("req", "ctx", None), P("req", "ctx", None))
    return jax.shard_map(
        per_device, mesh=mesh, in_specs=in_specs, out_specs=out_specs, check_vma=False
    )
```

profile of v0, /device:TPU:70, one launch (start us, length us, event | category | flops | bytes accessed | tf_op | source)
XLA Modules:
  0.0 350.5 jit_solution(10167611939933290079)
XLA Ops:
  7.2 3.5 copy.48
  10.7 1.6 slice_convert_fusion
  12.2 1.5 slice.171
  16.6 1.8 subtract_convert_fusion
  18.4 1.8 pad_maximum_fusion.2
  20.3 6.0 %all-to-all-start = ((bf16[128,8,1536]{0,2,1:T(8,128)(2,1)}), bf16[128,8,1536]{0,2,1:T(8,128)(2,1)S(1)}, u32[]{:S(2)}, u32[]{:S(2)}) async-start(bf16[128,8,1536]{0,2,1:T(8,128)(2,1)} %bitcast.92), calls=%async_computation | async-start | bytes 6291456 | tf_op jit(solution)/shard_map/all_to_all | solution.py:100
  33.7 1.9 compare_and_fusion
  36.8 49.1 %all-gather.4.cloned.1.call-done = bf16[1024,576]{0,1:T(8,128)(2,1)} async-done(((bf16[128,576]{0,1:T(8,128)(2,1)}), bf16[1024,576]{0,1:T(8,128)(2,1)}) %all-gather.4.cloned.1.call-update) | async-done | bytes 1179664 | tf_op jit(solution)/shard_map/all_gather | solution.py:93
  85.8 2.5 copy.50
  88.3 3.1 gather_fusion.1
  91.4 2.6 bitcast_select_fusion.2
  94.0 1.7 copy-done
  95.7 3.2 copy.49
  98.9 4.5 %reshape.395 = bf16[16,64,8,192]{3,2,1,0:T(8,128)(2,1)} reshape(bf16[8,128,1,1536]{3,1,0,2:T(8,128)(2,1)S(1)} %copy.49) | data formatting | bytes 6291456 | tf_op jit(solution)/shard_map/reshape | solution.py:106
  103.4 5.0 %gather_fusion = bf16[16,64,8,192]{3,2,1,0:T(8,128)(2,1)} fusion(bf16[16,64,8,192]{3,2,1,0:T(8,128)(2,1)} %reshape.395, s32[1024]{0:T(1024)S(1)} %pad_clamp_fusion.2), kind=kCustom, calls=%fused_computation | custom fusion | bytes 6291520 | tf_op jit(solution)/shard_map/jit(_take)/gather | solution.py:105
  108.4 6.6 %bitcast_select_fusion = bf16[1024,8,192]{2,1,0:T(8,128)(2,1)} fusion(bf16[16,64,8,192]{3,2,1,0:T(8,128)(2,1)} %gather_fusion, pred[1024]{0:T(1024)(128)(4,1)S(1)} %broadcast_in_dim.157), kind=kLoop, calls=%fused_computation.89 | loop fusion | flops 1572864 | bytes 6292480 | tf_op jit(solution)/shard_map/jit(_take)/select_n | solution.py:105
  115.0 6.5 %copy.51 = bf16[1024,8,192]{0,2,1:T(8,128)(2,1)} copy(bf16[1024,8,192]{2,1,0:T(8,128)(2,1)} %bitcast_select_fusion) | data formatting | bytes 6291456
  122.0 160.0 %while.11 = (s32[]{:T(128)}, bf16[8,1024,128]{2,1,0:T(8,128)(2,1)}, s32[1024]{0:T(1024)S(1)}, s32[]{:T(128)}, s32[8]{0:T(128)}, /*index=5*/bf16[1024,8,192]{0,2,...) while((s32[]{:T(128)}, bf16[8,1024,128]{2,1,0:T(8,128)(2,1)}, ...), condition=%wide.region_11.12_spmd.clone, body=%wide.region_2.11_spmd.clone.sunk | while | flops 1705772288 | bytes 23008316 | solution.py:138
  128.6 2.0 fusion.122
  132.0 2.1 fusion.119
  135.7 2.2 fusion.116
  139.6 1.7 fusion.113
  148.7 2.0 fusion.122
  152.1 2.1 fusion.119
  155.8 2.2 fusion.116
  159.7 1.6 fusion.113
  168.7 2.0 fusion.122
  172.1 2.1 fusion.119
  175.7 2.2 fusion.116
  179.7 1.6 fusion.113
  188.7 2.0 fusion.122
  192.1 2.1 fusion.119
  195.7 2.2 fusion.116
  199.7 1.6 fusion.113
  208.7 2.0 fusion.122
  212.1 2.1 fusion.119
  215.7 2.2 fusion.116
  219.7 1.6 fusion.113
  228.7 2.0 fusion.122
  232.1 2.1 fusion.119
  235.7 2.2 fusion.116
  239.7 1.6 fusion.113
  248.7 2.0 fusion.122
  252.1 2.1 fusion.119
  255.7 2.2 fusion.116
  259.7 1.6 fusion.113
  268.7 2.0 fusion.122
  272.0 2.1 fusion.119
  275.7 2.2 fusion.116
  279.7 1.6 fusion.113
  282.1 4.3 %copy.52 = bf16[1024,8,128]{2,1,0:T(8,128)(2,1)} copy(bf16[1024,8,128]{2,0,1:T(8,128)(2,1)} %bitcast.99) | data formatting | bytes 4194304 | tf_op jit(solution)/shard_map/transpose | solution.py:139
  286.4 2.8 reshape.397
  289.2 2.1 gather_fusion.2
  291.4 1.9 bitcast_select_fusion.1
  293.7 2.9 reduce.2
  296.6 6.3 %reshape.459 = bf16[8,2,65536]{2,1,0:T(2,128)(2,1)} reshape(bf16[1024,1024]{1,0:T(8,128)(2,1)} %reduce.2) | data formatting | bytes 4194304
  302.9 5.2 %all-to-all-start.1 = ((bf16[8,2,65536]{2,1,0:T(2,128)(2,1)}), bf16[8,2,65536]{2,1,0:T(2,128)(2,1)S(1)}, u32[]{:S(2)}, u32[]{:S(2)}) async-start(bf16[8,2,65536]{2,1,0:T(2,128)(2,1)} %reshape.459), calls=%async_computation.1 | async-start | bytes 4194304 | tf_op jit(solution)/shard_map/all_to_all | solution.py:141
  308.1 7.6 %reshape.457 = bf16[64,36864]{1,0:T(8,128)(2,1)} reshape(bf16[32,2,36864]{2,1,0:T(2,128)(2,1)} %all-gather.6.cloned.1.call-done) | data formatting | bytes 9437184
  315.7 3.9 %gather_fusion.3 = bf16[2,36864]{1,0:T(2,128)(2,1)S(1)} fusion(bf16[64,36864]{1,0:T(8,128)(2,1)} %reshape.457, s32[1024]{0:T(1024)} %pad_clamp_fusion), kind=kCustom, calls=%fused_computation.3 | custom fusion | bytes 294920 | tf_op jit(solution)/shard_map/jit(_take)/gather | solution.py:155
  320.5 9.3 %all-to-all-done.1 = bf16[8,2,65536]{2,1,0:T(2,128)(2,1)S(1)} async-done(((bf16[8,2,65536]{2,1,0:T(2,128)(2,1)}), bf16[8,2,65536]{2,1,0:T(2,128)(2,1)S(1)}, u32[]{:S(2)}, u32[]{:S(2)}) %all-to-all-start.1) | async-done | bytes 2097184 | tf_op jit(solution)/shard_map/all_to_all | solution.py:141
  329.8 4.4 %reshape.460 = bf16[1024,1,1024]{2,1,0:T(2,128)(2,1)} reshape(bf16[8,2,65536]{2,1,0:T(2,128)(2,1)S(1)} %all-to-all-done.1) | data formatting | bytes 4194304
  334.2 3.0 copy.57
  337.2 2.4 copy.54
  339.6 4.1 %copy.56 = bf16[1,128,8192]{2,1,0:T(8,128)(2,1)} copy(bf16[1,128,8192]{1,2,0:T(8,128)(2,1)} %bitcast.96) | data formatting | bytes 4194304
  (255 shorter events, 92.8 us)
Async XLA Ops:
  12.2 1.5 copy-start.11
  12.2 2.9 copy-start.6
  13.8 4.6 %copy-start.1 = (bf16[128,64,128]{0,2,1:T(8,128)(2,1)S(1)}, bf16[128,64,128]{0,2,1:T(8,128)(2,1)}, u32[]{:S(2)}) copy-start(bf16[128,64,128]{0,2,1:T(8,128)(2,1)} %slice.171) | copy-start | bytes 6291460
  20.2 6.1 %copy-start.9 = (f32[512]{0:T(512)S(1)}, f32[512]{0:T(512)}, u32[]{:S(2)}) copy-start(f32[512]{0:T(512)} %param.12) | copy-start | bytes 6148
  20.2 10.0 %copy-start.8 = (s32[32,2]{0,1:T(2,128)S(1)}, s32[32,2]{0,1:T(2,128)}, u32[]{:S(2)}) copy-start(s32[32,2]{0,1:T(2,128)} %param.17) | copy-start | bytes 772
  20.3 73.8 %all-to-all-start = ((bf16[128,8,1536]{0,2,1:T(8,128)(2,1)}), bf16[128,8,1536]{0,2,1:T(8,128)(2,1)S(1)}, u32[]{:S(2)}, u32[]{:S(2)}) async-start(bf16[128,8,1536]{0,2,1:T(8,128)(2,1)} %bitcast.92), calls=%async_computation | async-start | bytes 6291456 | tf_op jit(solution)/shard_map/all_to_all | solution.py:100
  26.2 59.6 %all-gather.4.cloned.1.call-start = ((), (), s32[]{:S(2)}) async-start(), calls=%async_computation.2 | async-start | bytes 1327104 | tf_op jit(solution)/shard_map/all_gather | solution.py:93
  27.2 280.9 %all-gather.6.cloned.1.call-start = ((), (), s32[]{:S(2)}) async-start(), calls=%async_computation.3 | async-start | bytes 4866048 | tf_op jit(solution)/shard_map/all_gather | solution.py:147
  94.0 1.7 copy-start
  115.0 7.0 %copy-start.2 = (bf16[1024,576]{1,0:T(8,128)(2,1)S(1)}, bf16[1024,576]{1,0:T(8,128)(2,1)}, u32[]{:S(2)}) copy-start(bf16[1024,576]{1,0:T(8,128)(2,1)} %bitcast_select_fusion.2) | copy-start | bytes 3538948
  139.6 1.8 copy-start.3
  139.6 1.8 copy-start.4
  139.6 1.8 copy-start.5
  159.7 1.7 copy-start.3
  159.7 1.7 copy-start.4
  159.7 1.7 copy-start.5
  179.7 1.7 copy-start.3
  179.7 1.7 copy-start.4
  179.7 1.7 copy-start.5
  199.7 1.7 copy-start.3
  199.7 1.7 copy-start.4
  199.7 1.7 copy-start.5
  219.7 1.7 copy-start.3
  219.7 1.7 copy-start.4
  219.7 1.7 copy-start.5
  239.6 1.7 copy-start.3
  239.7 1.7 copy-start.4
  239.7 1.7 copy-start.5
  259.6 1.7 copy-start.3
  259.6 1.7 copy-start.4
  259.7 1.7 copy-start.5
  279.6 1.7 copy-start.3
  279.6 1.7 copy-start.4
  279.6 1.7 copy-start.5
  289.2 2.1 copy-start.7
  302.9 26.9 %all-to-all-start.1 = ((bf16[8,2,65536]{2,1,0:T(2,128)(2,1)}), bf16[8,2,65536]{2,1,0:T(2,128)(2,1)S(1)}, u32[]{:S(2)}, u32[]{:S(2)}) async-start(bf16[8,2,65536]{2,1,0:T(2,128)(2,1)} %reshape.459), calls=%async_computation.1 | async-start | bytes 4194304 | tf_op jit(solution)/shard_map/all_to_all | solution.py:141
  308.1 11.6 %copy-start.10 = (pred[2]{0:T(512)(128)(4,1)S(1)}, pred[2]{0:T(512)(128)(4,1)}, u32[]{:S(2)}) copy-start(pred[2]{0:T(512)(128)(4,1)} %compare_and_fusion) | copy-start | bytes 10
Sparse Core Ops, SparseCore 0:
  29.3 56.4 all-gather.3
  88.4 62.6 all-gather.5
where the time goes:
time: 354 us; the launch traced here: 350 us
  local copies, waits for them, and re-layouts  94.6 us (27%)
  matrix products  92.1 us (26%)
  other arithmetic  62.8 us (18%)
  waiting for transfers between devices  58.4 us (16%)
  loops' own time  16.6 us (5%)
  between operations  14.9 us (4%)
  starting transfers between devices  11.2 us (3%)
    dot_general x32, matrix products, attend(): jnp.einsum('qc,dc->qd', output_latent, value_weight, preferred_element_ty...  63.3 us
    all_gather x1, waiting for transfers between devices, per_device(): key_rows = lax.all_gather(cache_rows, 'ctx', axis=0, tiled=True)  49.1 us
    unnamed x26, local copies, waits for them, and re-layouts  37.9 us
    dot_general x32, matrix products, attend(): jnp.einsum('qc,kc->qk', queries, key_rows, preferred_element_type=jnp.flo...  17.7 us
    another operation x1, loops' own time, per_device(): per_head = lax.map(one_head, jnp.arange(heads_here, dtype=jnp.int32))  16.6 us
    lt x24, other arithmetic, one_head(): key_pos[None, :] < length_here  15.6 us
    dot_general x8, matrix products, latent_query(): jnp.dot(head_queries[:, :HD], weight[:HD], preferred_element_type=jnp.flo...  11.1 us
    all_to_all x1, waiting for transfers between devices, per_device(): lax.all_to_all(as_sent(device_order), 'ctx', split_axis=0, concat_axis=1,...  9.26 us
  transfers between devices with their start and end apart: 4, of which 2 were waited for; matrix products, arithmetic and copies ran while one was open for 63% of the time, Pallas kernels for 0%

commit v1 on v0

v1 whole, which is shorter than its diff:
```python
import functools
import math

import jax
import jax.numpy as jnp
from jax import lax
from jax.experimental import pallas as pl
from jax.experimental.pallas import tpu as pltpu
from jax.sharding import PartitionSpec as P


HEADS = 64
HD = 128
ROPE = 64
LAT = 512
QW = HD + ROPE
PAIR = 2 * QW
BLK = 64
TILE = 256
GROUPS = 8
LOCAL = 2 * BLK
KVP = LAT + 128
PAGE = BLK * (LAT + ROPE) // 128

CHUNKS = 2
PAIRS = 4 // CHUNKS
QPART = PAIRS * PAIR
OPART = PAIRS * 2 * HD

theta_base = 10000.0
epsilon = 1e-06
masked_fill = -1e30
log2_scale = math.log2(math.e) * QW ** (-0.5)


NT = (((1,), (1,)), ((), ()))
SMEM = pl.BlockSpec(memory_space=pltpu.SMEM)
VMEM = pl.BlockSpec(memory_space=pltpu.VMEM)
ANY = pl.BlockSpec(memory_space=pl.ANY)

OFFSETS = ((0, 0), (0, 1), (0, 3), (1, 0), (1, 1), (1, 3), (0, 2), (1, 2))
BESIDE = {1: 4, 2: 5, 6: 7}
EARLY, LATE = (7, 4, 5, 3), (6, 1, 2)


def partner(context, k, back=False):
    dz, dy = OFFSETS[k]
    z, y = context // 4, context % 4
    step = 4 - dy if back else dy
    return ((z + dz) % 2) * 4 + (y + step) % 4


def forward(k):
    return [(d, partner(d, k)) for d in range(GROUPS)]


def params(limit):
    return pltpu.CompilerParams(vmem_limit_bytes=limit << 20)


def angle_table(positions):
    half = ROPE // 2
    frequency = jnp.exp(-math.log(theta_base) * jnp.arange(half, dtype=jnp.float32) / half)
    return positions.astype(jnp.float32)[:, None] * frequency[None, :]


def rotate_lanes(x, cosine, sine, lane):
    half = ROPE // 2
    swapped = jnp.where(lane % ROPE < half, pltpu.roll(x, 128 - half, 1), pltpu.roll(x, half, 1))
    return x * cosine + swapped * sine


def pack_kernel(chunk, partners, n_kv, *refs):
    ctx_ref, q_ref, *refs = refs
    kvs, refs = refs[:n_kv], refs[n_kv:]
    outs, (held, sems) = refs[: len(partners)], refs[len(partners) :]
    loads, stores = [], []
    for n, k in enumerate(partners):
        column = partner(ctx_ref[0], k) * (4 * PAIR) + chunk * QPART
        columns = pl.ds(pl.multiple_of(column, 128), QPART)
        loads.append(pltpu.make_async_copy(q_ref.at[0, :, columns], held.at[n], sems.at[0, n]))
        loads[-1].start()
    for n in range(len(partners)):
        for i, kv in enumerate(kvs):
            columns = pl.ds(QPART + i * KVP, KVP)
            stores.append(pltpu.make_async_copy(kv, outs[n].at[:, columns], sems.at[2 + i, n]))
            stores[-1].start()
    for n in range(len(partners)):
        loads[n].wait()
        stores.append(pltpu.make_async_copy(held.at[n], outs[n].at[:, :QPART], sems.at[1, n]))
        stores[-1].start()
    for store in stores:
        store.wait()


def pack(context, q_heads, chunk, partners, kvs=()):
    count = len(partners)
    outs = pl.pallas_call(
        functools.partial(pack_kernel, chunk, partners, len(kvs)),
        in_specs=[SMEM, ANY] + [VMEM] * len(kvs),
        out_specs=[ANY] * count,
        out_shape=[jax.ShapeDtypeStruct((LOCAL, QPART + len(kvs) * KVP), jnp.bfloat16)] * count,
        scratch_shapes=[
            pltpu.VMEM((count, LOCAL, QPART), jnp.bfloat16),
            pltpu.SemaphoreType.DMA((4, count)),
        ],
        compiler_params=params(8),
        name="pack",
    )(context, q_heads, *kvs)
    return dict(zip(partners, outs))


def pack_all_kernel(chunk, q_ref, o_ref, held, sems):
    loads, stores = [], []
    for j in range(GROUPS):
        columns = pl.ds(j * (4 * PAIR) + chunk * QPART, QPART)
        loads.append(pltpu.make_async_copy(q_ref.at[0, :, columns], held.at[j], sems.at[0, j]))
        loads[-1].start()
    for j in range(GROUPS):
        loads[j].wait()
        stores.append(pltpu.make_async_copy(held.at[j], o_ref.at[j], sems.at[1, j]))
        stores[-1].start()
    for store in stores:
        store.wait()


def pack_all(chunk, q_heads):
    shape = (GROUPS, LOCAL, QPART)
    return pl.pallas_call(
        functools.partial(pack_all_kernel, chunk),
        in_specs=[ANY],
        out_specs=ANY,
        out_shape=jax.ShapeDtypeStruct(shape, jnp.bfloat16),
        scratch_shapes=[pltpu.VMEM(shape, jnp.bfloat16), pltpu.SemaphoreType.DMA((2, GROUPS))],
        compiler_params=params(8),
        name="pack_all",
    )(q_heads)


def attend_kernel(first, *refs):
    ctx_ref, order_ref, length_ref, *refs = refs
    if first:
        arrived, refs = refs[:GROUPS], refs[GROUPS:]
        w_ref, cosines_ref, sines_ref, gain_ref, kv_ref, kvz_ref, o_ref, cs, krl, *refs = refs
    else:
        stacked, w_ref, cosines_ref, sines_ref, cs, krl, o_ref, *refs = refs
        arrived = [stacked.at[k] for k in range(GROUPS)]
    krr, cos_ref, sin_ref, *refs = refs
    qs, os, k0, k1, v = refs
    total = cs.shape[0]
    context = ctx_ref[0]

    if first:
        rows_of = {0: (kv_ref, 0), 3: (kvz_ref, 0)}
        for k, beyond in BESIDE.items():
            rows_of[k] = (arrived[k], QPART)
            rows_of[beyond] = (arrived[k], QPART + KVP)
    places = []
    for k in range(GROUPS):
        source = partner(context, k, back=True) if first else k
        for i in range(2):
            place = pl.multiple_of(order_ref[2 * source + i] * BLK, BLK)
            places.append((2 * source + i, place))
            here, there = slice(i * BLK, (i + 1) * BLK), pl.ds(place, BLK)
            for pair in range(PAIRS):
                qs[pair, there, :] = arrived[k][here, pair * PAIR : (pair + 1) * PAIR]
            if first:
                ref, at = rows_of[k]
                cs[there, :] = ref[here, at : at + LAT]
                krl[there, :] = ref[here, at + LAT : at + KVP]

    lane = lax.broadcasted_iota(jnp.int32, (TILE, 128), 1)
    for t in range(total // TILE):
        rows = slice(t * TILE, (t + 1) * TILE)
        cosine, sine = cosines_ref[:, rows].T, sines_ref[:, rows].T
        cosine = jnp.concatenate([cosine] * 4, axis=1)
        sine = jnp.concatenate([-sine, sine] * 2, axis=1)
        cos_ref[rows, :] = cosine
        sin_ref[rows, :] = sine
        if first:
            latent = cs[rows, :].astype(jnp.float32)
            mean_square = jnp.mean(latent * latent, axis=-1, keepdims=True)
            cs[rows, :] = (latent * lax.rsqrt(mean_square + epsilon) * gain_ref[...]).astype(jnp.bfloat16)
            turned = rotate_lanes(krl[rows, :].astype(jnp.float32), cosine, sine, lane)
            krl[rows, :] = turned.astype(jnp.bfloat16)
        else:
            turned = krl[rows, :].astype(jnp.float32)
        krr[rows, :] = pltpu.roll(turned, ROPE, 1).astype(jnp.bfloat16)

    length = length_ref[0]

    @pl.loop(0, PAIRS)
    def _(pair):
        gap = jnp.zeros((ROPE, LAT), jnp.bfloat16)
        w0, w1 = w_ref[2 * pair], w_ref[2 * pair + 1]
        wk = jnp.concatenate([w0[:HD], gap, w1[:HD], gap], axis=0)
        wv = jnp.concatenate([w0[HD:], w1[HD:]], axis=0)
        for t in range(total // TILE):
            rows = slice(t * TILE, (t + 1) * TILE)
            cache = cs[rows, :]
            kn = lax.dot_general(cache, wk, NT, preferred_element_type=jnp.float32).astype(jnp.bfloat16)
            k0[rows, :128] = kn[:, :128]
            k0[rows, 128:] = krl[rows, :]
            k1[rows, :128] = kn[:, 128:256]
            k1[rows, 128:] = kn[:, 256:] + krr[rows, :]
            v[rows, :] = lax.dot_general(cache, wv, NT, preferred_element_type=jnp.float32).astype(jnp.bfloat16)
        for t in range(total // TILE):
            rows = slice(t * TILE, (t + 1) * TILE)
            keys = (t + 1) * TILE
            cosine, sine = cos_ref[rows, :], sin_ref[rows, :]
            one = qs[pair, rows, 128:256].astype(jnp.float32)
            two = qs[pair, rows, 256:].astype(jnp.float32)
            one = jnp.where(lane < ROPE, rotate_lanes(one, cosine, sine, lane), one).astype(jnp.bfloat16)
            two = jnp.where(lane < ROPE, two, rotate_lanes(two, cosine, sine, lane)).astype(jnp.bfloat16)
            queries = (jnp.concatenate([qs[pair, rows, :128], one], axis=1), jnp.concatenate([one, two], axis=1))
            row = lax.broadcasted_iota(jnp.int32, (TILE, TILE), 0)
            column = lax.broadcasted_iota(jnp.int32, (TILE, TILE), 1)
            valid = lax.broadcasted_iota(jnp.int32, (TILE, HD), 0) + t * TILE < length
            for head, k in ((0, k0), (1, k1)):
                s = lax.dot_general(queries[head], k[:keys, :], NT, preferred_element_type=jnp.float32)
                last = jnp.where(column <= row, s[:, keys - TILE :], masked_fill)
                s = last if t == 0 else jnp.concatenate([s[:, : keys - TILE], last], axis=1)
                top = jnp.max(s, axis=1, keepdims=True)
                p = jnp.exp2((s - top) * log2_scale)
                bottom = jnp.sum(p, axis=1, keepdims=True)
                side = slice(head * HD, (head + 1) * HD)
                o = jnp.dot(p.astype(jnp.bfloat16), v[:keys, side], preferred_element_type=jnp.float32)
                os[pair, rows, side] = jnp.where(valid, o / bottom, 0.0).astype(jnp.bfloat16)

    for block, place in places:
        for pair in range(PAIRS):
            o_ref[block, :, pair * 2 * HD : (pair + 1) * 2 * HD] = os[pair, pl.ds(place, BLK), :]


def attend(chunk, context, order_row, length, arrived, kv_up, extra):
    first = chunk == 0
    total = GROUPS * LOCAL
    whole = lambda a: pl.BlockSpec(a.shape, lambda i: (0,) * a.ndim)
    out = jax.ShapeDtypeStruct((2 * GROUPS, BLK, OPART), jnp.bfloat16)
    kept = [((total, LAT), jnp.bfloat16), ((total, 128), jnp.bfloat16)]
    outs = [out] + [jax.ShapeDtypeStruct(*one) for one in kept] * first
    outs = pl.pallas_call(
        functools.partial(attend_kernel, first),
        grid=(1,),
        in_specs=[SMEM, SMEM, SMEM]
        + [whole(a) for a in arrived]
        + [pl.BlockSpec((2 * PAIRS, 2 * HD, LAT), lambda i: (chunk, 0, 0))]
        + [whole(a) for a in extra],
        out_specs=[whole(a) for a in outs],
        out_shape=outs,
        scratch_shapes=[
            pltpu.VMEM((total, 128), jnp.bfloat16),
            pltpu.VMEM((total, 128), jnp.float32),
            pltpu.VMEM((total, 128), jnp.float32),
            pltpu.VMEM((PAIRS, total, PAIR), jnp.bfloat16),
            pltpu.VMEM((PAIRS, total, 2 * HD), jnp.bfloat16),
            pltpu.VMEM((total, 256), jnp.bfloat16),
            pltpu.VMEM((total, 256), jnp.bfloat16),
            pltpu.VMEM((total, 256), jnp.bfloat16),
        ],
        compiler_params=params(60),
        cost_estimate=pl.CostEstimate(
            flops=PAIRS * 2_200_000_000, bytes_accessed=6_000_000, transcendentals=PAIRS * 1_300_000
        ),
        name="attend",
    )(context, order_row, length, *arrived, kv_up, *extra)
    return outs[0].reshape(GROUPS, LOCAL, OPART), outs[1:]


def unpack_kernel(chunk, part_ref, *refs):
    o_ref, sems = refs[-2:]
    stores = []
    for j in range(GROUPS):
        columns = pl.ds(j * (8 * HD) + chunk * OPART, OPART)
        stores.append(pltpu.make_async_copy(part_ref.at[j], o_ref.at[0, :, columns], sems.at[j]))
        stores[-1].start()
    for store in stores:
        store.wait()


def unpack(chunk, part, out):
    more = [] if out is None else [out]
    return pl.pallas_call(
        functools.partial(unpack_kernel, chunk),
        in_specs=[VMEM] + [ANY] * len(more),
        out_specs=ANY,
        out_shape=jax.ShapeDtypeStruct((1, LOCAL, HEADS * HD), jnp.bfloat16),
        scratch_shapes=[pltpu.SemaphoreType.DMA((GROUPS,))],
        input_output_aliases={1: 0} if more else {},
        compiler_params=params(8),
        name="unpack",
    )(part, *more)


def pages_kernel(ctx_ref, order_ref, offset_ref, kv_ref, gain_ref, freq_ref, o_ref, rows, page):
    row = lax.broadcasted_iota(jnp.int32, (LOCAL, 128), 0)
    lane = lax.broadcasted_iota(jnp.int32, (LOCAL, 128), 1)
    first, second = order_ref[2 * ctx_ref[0]], order_ref[2 * ctx_ref[0] + 1]
    position = jnp.where(row < BLK, first, second) * BLK + row % BLK + offset_ref[0]
    angles = position.astype(jnp.float32) * freq_ref[...]
    sine = jnp.sin(angles)
    latent = kv_ref[:, :LAT].astype(jnp.float32)
    mean_square = jnp.mean(latent * latent, axis=-1, keepdims=True)
    normed = latent * lax.rsqrt(mean_square + epsilon) * gain_ref[...]
    for t in range(4):
        rows[t] = normed[:, 128 * t : 128 * (t + 1)].astype(jnp.bfloat16).astype(jnp.float32)
    rope = kv_ref[:, LAT:].astype(jnp.float32)
    rope = rotate_lanes(rope, jnp.cos(angles), jnp.where(lane % ROPE < ROPE // 2, -sine, sine), lane)
    rows[4] = rope.astype(jnp.bfloat16).astype(jnp.float32)
    half = BLK // 2
    left = lax.broadcasted_iota(jnp.int32, (half, 128), 1) < ROPE
    for i in range(2):
        even = [rows[t, pl.ds(i * BLK, half, stride=2), :] for t in range(5)]
        odd = [pltpu.roll(rows[t, pl.ds(i * BLK + 1, half, stride=2), :], ROPE, 1) for t in range(5)]
        for t in range(9):
            if t < 4:
                tile = even[t]
            elif t == 4:
                tile = jnp.where(left, even[4], odd[0])
            else:
                tile = jnp.where(left, odd[t - 5], odd[t - 4])
            page[pl.ds(t, half, stride=9), :] = tile
        o_ref[i] = page[...].astype(jnp.bfloat16)


def make_pages(context, order_row, offsets, kv, gain):
    half = ROPE // 2
    lane = jnp.arange(128) % half
    freq = jnp.exp(-math.log(theta_base) * lane.astype(jnp.float32) / half)
    return pl.pallas_call(
        pages_kernel,
        in_specs=[SMEM] * 3 + [VMEM] * 3,
        out_specs=VMEM,
        out_shape=jax.ShapeDtypeStruct((2, PAGE, 128), jnp.bfloat16),
        scratch_shapes=[pltpu.VMEM((5, LOCAL, 128), jnp.float32), pltpu.VMEM((PAGE, 128), jnp.float32)],
        compiler_params=params(8),
        name="pages",
    )(context, order_row, offsets, kv, gain, freq[None])


def merge_kernel(one_ref, two_ref, o_ref):
    o_ref[:2] = one_ref[...]
    o_ref[2:] = two_ref[...]


def merge(one, two):
    return pl.pallas_call(
        merge_kernel,
        in_specs=[VMEM] * 2,
        out_specs=VMEM,
        out_shape=jax.ShapeDtypeStruct((4, PAGE, 128), jnp.bfloat16),
        compiler_params=params(8),
        name="merge",
    )(one, two)


def relay_kernel(req_ref, owners_ref, table_ref, *refs):
    parts, (o_ref, final_ref, table, count, sems) = refs[:4], refs[4:]
    me = req_ref[0]
    my_x, my_z, my_core = me // 8, (me // 2) % 4, me % 2
    for i in range(8):
        table[i] = 0
    for i in range(4):
        count[i] = 0
    for x in range(4):
        back = (my_x + 4 - x) % 4
        for core in range(2):
            for page in range(2):
                owner = owners_ref[page, request(x, my_z, core)]

                @pl.when((owner // 8 == my_x) & (owner % 2 == my_core))
                def _():
                    turn = ((owner // 2) % 4 + 4 - my_z) % 4
                    slot = count[turn]
                    table[2 * turn + jnp.minimum(slot, 1)] = 4 * back + 2 * (core ^ my_core) + page
                    count[turn] = slot + 1

    for i in range(8):
        for d, part in enumerate(parts):

            @pl.when(table[i] // 4 == d)
            def _():
                pltpu.make_async_copy(part.at[table[i] % 4], o_ref.at[i], sems.at[i]).start()

    owner = table_ref[...]
    flat = 2 * lax.broadcasted_iota(jnp.int32, owner.shape, 1) + lax.broadcasted_iota(jnp.int32, owner.shape, 0)
    first = jnp.min(jnp.where(owner == me, flat, 4 * owner.shape[1]))
    last = jnp.max(jnp.where(owner == me, flat, 0))
    first = jnp.minimum(first, last)
    turn_first = (my_z + 4 - (first // 4) % 4) % 4
    turn_last = (my_z + 4 - (last // 4) % 4) % 4
    final_ref[0] = 2 * turn_first
    final_ref[1] = 2 * turn_last + jnp.where(turn_first == turn_last, 1, 0)
    for i in range(8):
        pltpu.make_async_copy(parts[0].at[0], o_ref.at[i], sems.at[i]).wait()


def relay_pages(req, owners, parts):
    page = parts[0].shape[1:]
    return pl.pallas_call(
        relay_kernel,
        in_specs=[SMEM, SMEM, VMEM] + [ANY] * 4,
        out_specs=[VMEM, SMEM],
        out_shape=[
            jax.ShapeDtypeStruct((8,) + page, parts[0].dtype),
            jax.ShapeDtypeStruct((2,), jnp.int32),
        ],
        scratch_shapes=[
            pltpu.SMEM((8,), jnp.int32),
            pltpu.SMEM((4,), jnp.int32),
            pltpu.SemaphoreType.DMA((8,)),
        ],
        compiler_params=params(8),
        name="relay_pages",
    )(req, owners, owners, *parts)


def keep_kernel(final_ref, *refs):
    o_ref = refs[-1]
    for i in range(2):
        for turn, ref in enumerate(refs[:-1]):

            @pl.when(final_ref[i] // 2 == turn)
            def _():
                o_ref[i] = ref[final_ref[i] % 2]


def keep_pages(final, parts):
    return pl.pallas_call(
        keep_kernel,
        in_specs=[SMEM] + [VMEM] * len(parts),
        out_specs=VMEM,
        out_shape=jax.ShapeDtypeStruct(parts[0].shape, parts[0].dtype),
        compiler_params=params(8),
        name="keep_pages",
    )(final, *parts)


def request(x, z, core):
    return (x * 4 + z) * 2 + core


EACH = [(x, z, c) for x in range(4) for z in range(4) for c in range(2)]


def along_x(d):
    return [(request(x, z, c), request((x + d) % 4, z, c)) for x, z, c in EACH]


def along_z(d):
    return [(request(x, z, c), request(x, (z + d) % 4, c)) for x, z, c in EACH]


def ship(pages, owners):
    other = lax.ppermute(pages, "req", [(request(x, z, c), request(x, z, 1 - c)) for x, z, c in EACH])
    both = merge(pages, other)
    parts = [both] + [None] * 3
    for d in (1, 3, 2):
        parts[d] = lax.ppermute(both, "req", along_x(d))
    outgoing, final = relay_pages(lax.axis_index("req").reshape(1), owners.T, parts)
    arrived = [outgoing[:2]] + [lax.ppermute(outgoing[2 * d : 2 * d + 2], "req", along_z(d)) for d in (1, 2, 3)]
    return keep_pages(final, arrived)


def exchange(array):
    return lax.all_to_all(array, "ctx", split_axis=0, concat_axis=0, tiled=True)


def body(q_heads, kv_latent, latent_gain, kv_up, offsets, lengths, block_order, owners):
    context = lax.axis_index("ctx").reshape(1)
    order_row = block_order[0]
    gain = latent_gain[None]
    padded = jnp.pad(kv_latent[0], ((0, 0), (0, KVP - kv_latent.shape[2])))
    beyond = lax.ppermute(padded, "ctx", forward(3))

    sent = pack(context, q_heads, 0, (0,) + EARLY)
    pages = make_pages(context, order_row, offsets, padded, gain)
    shipped = ship(pages, owners).reshape(1, 2, PAGE * 128)
    sent.update(pack(context, q_heads, 0, LATE, (padded, beyond)))
    arrived = [[sent[0]] + [lax.ppermute(sent[k], "ctx", forward(k)) for k in range(1, GROUPS)]]
    for chunk in range(1, CHUNKS):
        arrived.append([exchange(pack_all(chunk, q_heads))])
    offsets, _ = lax.optimization_barrier((offsets, sent[1]))
    angles = angle_table(offsets[0] + jnp.arange(GROUPS * LOCAL, dtype=jnp.int32)).T
    extra = [jnp.cos(angles), jnp.sin(angles), gain, padded, beyond]
    attn_out = None
    for chunk in range(CHUNKS):
        out, kept = attend(chunk, context, order_row, lengths, arrived[chunk], kv_up, extra)
        extra = extra[:2] + list(kept) if chunk == 0 else extra
        attn_out = unpack(chunk, exchange(out), attn_out)
    return attn_out, shipped


def solution(mesh):
    in_specs = (
        P("req", "ctx", None),
        P("req", "ctx", None),
        P(),
        P("ctx", None, None),
        P("req"),
        P("req"),
        P("req", None),
        P(None, "ctx"),
    )
    out_specs = (P("req", "ctx", None), P("req", "ctx", None))
    return jax.shard_map(body, mesh=mesh, in_specs=in_specs, out_specs=out_specs, check_vma=False)
```

time: 354 us -> 157 us (0.44)
  the two profiles are of different devices: /device:TPU:70 before, /device:TPU:1 now
where the time goes in v1:
time: 157 us
  waiting for transfers between devices  67.2 us (43%)
  starting transfers between devices  43.4 us (28%)
  Pallas kernels  37.3 us (24%)
  local copies, waits for them, and re-layouts  5.51 us (4%)
  between operations  2.36 us (2%)
    pallas_call x2, Pallas kernels, attend(): pl.pallas_call(functools.partial(attend_kernel, first), grid=(1,), in_spe...  25.9 us
    ppermute x7, waiting for transfers between devices, body(): lax.ppermute(sent[k], 'ctx', forward(k))  20.6 us
    ppermute x1, waiting for transfers between devices, body(): beyond = lax.ppermute(padded, 'ctx', forward(3))  20.2 us
    all_to_all x3, starting transfers between devices, exchange(): return lax.all_to_all(array, 'ctx', split_axis=0, concat_axis=0, tiled=True)  15.7 us
    ppermute x3, waiting for transfers between devices, ship(): lax.ppermute(outgoing[2 * d:2 * d + 2], 'req', along_z(d))  13 us
    ppermute x3, waiting for transfers between devices, ship(): parts[d] = lax.ppermute(both, 'req', along_x(d))  12.4 us
    ppermute x3, starting transfers between devices, ship(): lax.ppermute(outgoing[2 * d:2 * d + 2], 'req', along_z(d))  9.79 us
    ppermute x7, starting transfers between devices, body(): lax.ppermute(sent[k], 'ctx', forward(k))  8.14 us
  transfers between devices with their start and end apart: 18, of which 12 were waited for; matrix products, arithmetic and copies ran while one was open for 1% of the time, Pallas kernels for 22%

profile of v1, /device:TPU:1, one launch (start us, length us, event | category | flops | bytes accessed | tf_op | source)
XLA Modules:
  0.0 157.0 jit_solution(5607786860738061061)
XLA Ops:
  0.6 0.0 copy-start
  0.6 1.9 %copy-done = bf16[1,128,12288]{2,1,0:T(8,128)(2,1)S(1)} copy-done((bf16[1,128,12288]{2,1,0:T(8,128)(2,1)S(1)}, bf16[1,128,12288]{2,1,0:T(8,128)(2,1)}, u32[]{:S(2)}) %copy-start) | copy-done | bytes 3145752
  2.5 2.4 %pack_all.1 = bf16[8,128,768]{2,1,0:T(8,128)(2,1)S(1)} custom-call(bf16[1,128,12288]{2,1,0:T(8,128)(2,1)S(1)} %copy-done), custom_call_target="tpu_custom_call" | custom-call | tf_op jit(solution)/shard_map/pack_all/pallas_call | solution.py:129
  4.9 0.0 copy-start.2
  5.0 1.1 copy-done.2
  6.1 6.6 %all-to-all-start = ((bf16[8,128,768]{2,1,0:T(8,128)(2,1)}), bf16[8,128,768]{2,1,0:T(8,128)(2,1)}, u32[]{:S(2)}, u32[]{:S(2)}) async-start(bf16[8,128,768]{2,1,0:T(8,128)(2,1)} %copy-done.2), calls=%async_computation | async-start | bytes 3145728 | tf_op jit(solution)/shard_map/all_to_all | solution.py:466
  12.7 0.0 copy-done.10
  12.7 0.2 copy.11
  12.9 0.0 copy-start.3
  12.9 1.5 collective-permute-start
  14.5 20.2 %collective-permute-done.refs_3_.refs_16_ = bf16[128,640]{1,0:T(8,128)(2,1)S(1)} collective-permute-done((bf16[128,640]{1,0:T(8,128)(2,1)S(1)}, bf16[128,640]{1,0:T(8,128)(2,1)S(1)}, u32[]{:S(2)}, u32[]{:S(2)}) %collective-permute-start) | collective-permute-done | bytes 163872 | tf_op jit(solution)/shard_map/ppermute | solution.py:474
  34.6 0.0 copy-done.1
  34.6 0.4 pack.2
  35.1 1.3 collective-permute-start.1
  36.3 1.6 collective-permute-start.2
  37.9 1.4 collective-permute-start.6
  39.3 1.7 %pack.3 = (bf16[128,768]{1,0:T(8,128)(2,1)S(1)}, bf16[128,768]{1,0:T(8,128)(2,1)S(1)}, bf16[128,768]{1,0:T(8,128)(2,1)S(1)}, bf16[128,768]{1,0:T(8,128)(2,1)S(1)}, bf16[128,768]{1,0:T(8,128)(2,1)S(1)}) custom-call(s32[1]{0:T(128)} %bitcast.refs_0_.ctx_ref, bf16[1,128,12288]{2,1,0:T(8,128)(2,1)S(1)} %copy-done.1), custom_call_target="tpu_custom_call" | custom-call | tf_op jit(solution)/shard_map/pack/pallas_call | solution.py:98
  41.0 0.0 copy-done.3
  41.0 0.0 copy-done.5
  41.0 0.7 copy-done.9
  41.7 0.3 collective-permute-start.3
  41.9 1.5 collective-permute-start.4
  44.7 1.8 %collective-permute-done.3.refs_6_ = bf16[128,768]{1,0:T(8,128)(2,1)S(1)} collective-permute-done((bf16[128,768]{1,0:T(8,128)(2,1)S(1)}, bf16[128,768]{1,0:T(8,128)(2,1)S(1)}, u32[]{:S(2)}, u32[]{:S(2)}) %collective-permute-start.3) | collective-permute-done | bytes 196640 | tf_op jit(solution)/shard_map/ppermute | solution.py:480
  46.5 0.8 collective-permute-start.5
  47.3 2.7 %collective-permute-done.4.refs_7_ = bf16[128,768]{1,0:T(8,128)(2,1)S(1)} collective-permute-done((bf16[128,768]{1,0:T(8,128)(2,1)S(1)}, bf16[128,768]{1,0:T(8,128)(2,1)S(1)}, u32[]{:S(2)}, u32[]{:S(2)}) %collective-permute-start.4) | collective-permute-done | bytes 196640 | tf_op jit(solution)/shard_map/ppermute | solution.py:480
  50.1 1.4 collective-permute-start.7
  51.4 1.2 multiply_sine_fusion
  52.6 1.7 %collective-permute-done.5.refs_8_ = bf16[128,768]{1,0:T(8,128)(2,1)S(1)} collective-permute-done((bf16[128,768]{1,0:T(8,128)(2,1)S(1)}, bf16[128,768]{1,0:T(8,128)(2,1)S(1)}, u32[]{:S(2)}, u32[]{:S(2)}) %collective-permute-start.5) | collective-permute-done | bytes 196640 | tf_op jit(solution)/shard_map/ppermute | solution.py:480
  54.3 4.9 %collective-permute-done.7.refs_10_ = bf16[128,768]{1,0:T(8,128)(2,1)S(1)} collective-permute-done((bf16[128,768]{1,0:T(8,128)(2,1)S(1)}, bf16[128,768]{1,0:T(8,128)(2,1)S(1)}, u32[]{:S(2)}, u32[]{:S(2)}) %collective-permute-start.7) | collective-permute-done | bytes 196640 | tf_op jit(solution)/shard_map/ppermute | solution.py:480
  59.2 0.0 collective-permute-done.1.refs_4_
  59.2 0.0 collective-permute-done.2.refs_5_
  59.2 0.0 copy-start.12
  59.3 9.5 %collective-permute-done.6.refs_9_ = bf16[128,2048]{1,0:T(8,128)(2,1)S(1)} collective-permute-done((bf16[128,2048]{1,0:T(8,128)(2,1)S(1)}, bf16[128,2048]{1,0:T(8,128)(2,1)S(1)}, u32[]{:S(2)}, u32[]{:S(2)}) %collective-permute-start.6) | collective-permute-done | bytes 524320 | tf_op jit(solution)/shard_map/ppermute | solution.py:480
  68.8 0.8 copy-done.13
  69.7 0.0 copy-done.15
  69.7 0.0 copy-done.17
  69.7 13.6 %attend.2 = (bf16[16,64,512]{2,1,0:T(8,128)(2,1)}, bf16[1024,512]{1,0:T(8,128)(2,1)}, bf16[1024,128]{1,0:T(8,128)(2,1)}) custom-call(s32[1]{0:T(128)} %bitcast.refs_0_.ctx_ref, s32[16]{0:T(128)} %bitcast.14, s32[1]{0:T(128)S(6)} %copy.14.refs_2_, bf16[128,768]{1,0:T(8,128)(2,1)} %copy-done.9, bf16[128,2048]{1,0:T(8,128)(2,1)} %copy-done.11, ...), custom_call_target="tpu_custom_call" | custom-call | flops 4400000000 | bytes 6000000 | tf_op jit(solution)/shard_map/attend/pallas_call | solution.py:242
  83.2 0.0 all-to-all-done.refs_3_
  83.3 3.6 %all-to-all-start.2 = ((bf16[8,128,512]{2,1,0:T(8,128)(2,1)}), bf16[8,128,512]{2,1,0:T(8,128)(2,1)S(1)}, u32[]{:S(2)}, u32[]{:S(2)}) async-start(bf16[8,128,512]{2,1,0:T(8,128)(2,1)} %bitcast.18), calls=%async_computation.2 | async-start | bytes 2097152 | tf_op jit(solution)/shard_map/all_to_all | solution.py:466
  86.8 12.3 %attend.3 = bf16[16,64,512]{2,1,0:T(8,128)(2,1)} custom-call(s32[1]{0:T(128)} %bitcast.refs_0_.ctx_ref, s32[16]{0:T(128)} %bitcast.15, s32[1]{0:T(128)S(6)} %copy.14.refs_2_, bf16[8,128,768]{2,1,0:T(8,128)(2,1)} %all-to-all-done.refs_3_, bf16[8,256,512]{2,1,0:T(8,128)(2,1)} %refs_4_.1, f32[32,1024]{1,0:T(8,128)} %get-tuple-element.35.refs_12_.refs_5_, ...), custom_call_target="tpu_custom_call" | custom-call | flops 4400000000 | bytes 6000000 | tf_op jit(solution)/shard_map/attend/pallas_call | solution.py:242
  99.1 0.0 copy-start.6
  99.1 0.0 all-to-all-done.2.part_ref
  99.1 5.6 %all-to-all-start.1 = ((bf16[8,128,512]{2,1,0:T(8,128)(2,1)}), bf16[8,128,512]{2,1,0:T(8,128)(2,1)S(1)}, u32[]{:S(2)}, u32[]{:S(2)}) async-start(bf16[8,128,512]{2,1,0:T(8,128)(2,1)} %bitcast.17), calls=%async_computation.1 | async-start | bytes 2097152 | tf_op jit(solution)/shard_map/all_to_all | solution.py:466
  104.7 1.0 pages.1.one_ref
  105.7 3.7 %collective-permute-start.8 = (bf16[2,288,128]{2,1,0:T(8,128)(2,1)S(1)}, bf16[2,288,128]{2,1,0:T(8,128)(2,1)S(1)}, u32[]{:S(2)}, u32[]{:S(2)}) collective-permute-start(bf16[2,288,128]{2,1,0:T(8,128)(2,1)S(1)} %pages.1.one_ref), channel_id=1, source_target_pairs={{0,8},{8,0},{16,24},{24,16},{32,40},{40,32},{48,56},{56,48},{64,72... | collective-permute-start | bytes 442376 | tf_op jit(solution)/shard_map/ppermute | solution.py:455
  109.4 1.0 collective-permute-done.8.two_ref
  110.5 3.0 %collective-permute-start.10 = (bf16[4,288,128]{2,1,0:T(8,128)(2,1)S(1)}, bf16[4,288,128]{2,1,0:T(8,128)(2,1)S(1)}, u32[]{:S(2)}, u32[]{:S(2)}) collective-permute-start(bf16[4,288,128]{2,1,0:T(8,128)(2,1)S(1)} %merge.1.refs_0_), channel_id=1, source_target_pairs={{0,128},{8,136},{16,144},{24,152},{32,160},{40,168},{48,176},{56,1... | collective-permute-start | bytes 884744 | tf_op jit(solution)/shard_map/ppermute | solution.py:459
  113.4 0.9 collective-permute-start.11
  114.3 0.6 collective-permute-start.9
  114.9 5.4 %collective-permute-done.10.refs_2_ = bf16[4,288,128]{2,1,0:T(8,128)(2,1)S(1)} collective-permute-done((bf16[4,288,128]{2,1,0:T(8,128)(2,1)S(1)}, bf16[4,288,128]{2,1,0:T(8,128)(2,1)S(1)}, u32[]{:S(2)}, u32[]{:S(2)}) %collective-permute-start.10) | collective-permute-done | bytes 294944 | tf_op jit(solution)/shard_map/ppermute | solution.py:459
  120.3 6.5 %collective-permute-done.11.refs_3_ = bf16[4,288,128]{2,1,0:T(8,128)(2,1)S(1)} collective-permute-done((bf16[4,288,128]{2,1,0:T(8,128)(2,1)S(1)}, bf16[4,288,128]{2,1,0:T(8,128)(2,1)S(1)}, u32[]{:S(2)}, u32[]{:S(2)}) %collective-permute-start.11) | collective-permute-done | bytes 294944 | tf_op jit(solution)/shard_map/ppermute | solution.py:459
  126.8 0.5 collective-permute-done.9.refs_1_
  127.3 3.2 %relay_pages.1 = (bf16[8,288,128]{2,1,0:T(8,128)(2,1)S(1)}, s32[2]{0:T(128)S(1)}) custom-call(s32[1]{0:T(128)} %bitcast.7.req_ref, s32[2,32]{1,0:T(2,128)S(1)} %bitcast.10, s32[2,32]{1,0:T(2,128)S(1)} %bitcast.11, bf16[4,288,128]{2,1,0:T(8,128)(2,1)S(1)} %merge.1.refs_0_, bf16[4,288,128]{2,1,0:T(8,128)(2,1)S(1)} %collective-permute-done.9.refs_1_, ...), custom_call_target="tpu_custom_call" | custom-call | tf_op jit(solution)/shard_map/relay_pages/pallas_call | solution.py:400
  130.6 3.2 %collective-permute-start.12 = (bf16[2,288,128]{2,1,0:T(8,128)(2,1)S(1)}, bf16[2,288,128]{2,1,0:T(8,128)(2,1)S(1)}, u32[]{:S(2)}, u32[]{:S(2)}) collective-permute-start(bf16[2,288,128]{2,1,0:T(8,128)(2,1)S(1)} %get-tuple-element.32), channel_id=1, source_target_pairs={{0,16},{8,24},{16,32},{24,40},{32,48},{40,56},{48,0},{56,8},{64,80... | collective-permute-start | bytes 442376 | tf_op jit(solution)/shard_map/ppermute | solution.py:461
  133.8 4.2 %collective-permute-start.13 = (bf16[2,288,128]{2,1,0:T(8,128)(2,1)S(1)}, bf16[2,288,128]{2,1,0:T(8,128)(2,1)S(1)}, u32[]{:S(2)}, u32[]{:S(2)}) collective-permute-start(bf16[2,288,128]{2,1,0:T(8,128)(2,1)S(1)} %get-tuple-element.31), channel_id=1, source_target_pairs={{0,32},{8,40},{16,48},{24,56},{32,0},{40,8},{48,16},{56,24},{64,96... | collective-permute-start | bytes 442376 | tf_op jit(solution)/shard_map/ppermute | solution.py:461
  138.0 2.4 %collective-permute-start.14 = (bf16[2,288,128]{2,1,0:T(8,128)(2,1)S(1)}, bf16[2,288,128]{2,1,0:T(8,128)(2,1)S(1)}, u32[]{:S(2)}, u32[]{:S(2)}) collective-permute-start(bf16[2,288,128]{2,1,0:T(8,128)(2,1)S(1)} %get-tuple-element.30), channel_id=1, source_target_pairs={{0,48},{8,56},{16,0},{24,8},{32,16},{40,24},{48,32},{56,40},{64,11... | collective-permute-start | bytes 442376 | tf_op jit(solution)/shard_map/ppermute | solution.py:461
  140.3 0.0 collective-permute-done.12.refs_1_
  140.4 5.2 %collective-permute-done.13.refs_2_ = bf16[2,288,128]{2,1,0:T(8,128)(2,1)S(1)} collective-permute-done((bf16[2,288,128]{2,1,0:T(8,128)(2,1)S(1)}, bf16[2,288,128]{2,1,0:T(8,128)(2,1)S(1)}, u32[]{:S(2)}, u32[]{:S(2)}) %collective-permute-start.13) | collective-permute-done | bytes 147488 | tf_op jit(solution)/shard_map/ppermute | solution.py:461
  145.5 7.8 %collective-permute-done.14.refs_3_ = bf16[2,288,128]{2,1,0:T(8,128)(2,1)S(1)} collective-permute-done((bf16[2,288,128]{2,1,0:T(8,128)(2,1)S(1)}, bf16[2,288,128]{2,1,0:T(8,128)(2,1)S(1)}, u32[]{:S(2)}, u32[]{:S(2)}) %collective-permute-start.14) | collective-permute-done | bytes 147488 | tf_op jit(solution)/shard_map/ppermute | solution.py:461
  153.3 0.7 keep_pages.1
  154.0 0.7 reshape.64
  154.7 1.0 unpack.2.refs_0_
  155.8 0.0 all-to-all-done.1.part_ref
  155.8 1.0 unpack.3
  (27 shorter events, 0.1 us)
Async XLA Ops:
  0.6 1.9 %copy-start = (bf16[1,128,12288]{2,1,0:T(8,128)(2,1)S(1)}, bf16[1,128,12288]{2,1,0:T(8,128)(2,1)}, u32[]{:S(2)}) copy-start(bf16[1,128,12288]{2,1,0:T(8,128)(2,1)} %refs_1_.3) | copy-start | bytes 9437188
  2.5 10.2 %copy-start.10 = (bf16[1,128,576]{1,2,0:T(8,128)(2,1)S(1)}, bf16[1,128,576]{1,2,0:T(8,128)(2,1)}, u32[]{:S(2)}) copy-start(bf16[1,128,576]{1,2,0:T(8,128)(2,1)} %param.9) | copy-start | bytes 442372
  4.9 1.1 copy-start.2
  6.1 28.5 %copy-start.1 = (bf16[1,128,12288]{2,1,0:T(8,128)(2,1)S(1)}, bf16[1,128,12288]{2,1,0:T(8,128)(2,1)}, u32[]{:S(2)}) copy-start(bf16[1,128,12288]{2,1,0:T(8,128)(2,1)} %refs_1_.3) | copy-start | bytes 9437188
  6.1 77.2 %all-to-all-start = ((bf16[8,128,768]{2,1,0:T(8,128)(2,1)}), bf16[8,128,768]{2,1,0:T(8,128)(2,1)}, u32[]{:S(2)}, u32[]{:S(2)}) async-start(bf16[8,128,768]{2,1,0:T(8,128)(2,1)} %copy-done.2), calls=%async_computation | async-start | bytes 3145728 | tf_op jit(solution)/shard_map/all_to_all | solution.py:466
  12.9 28.1 %copy-start.3 = (bf16[128,640]{1,0:T(8,128)(2,1)}, bf16[128,640]{1,0:T(8,128)(2,1)S(1)}, u32[]{:S(2)}) copy-start(bf16[128,640]{1,0:T(8,128)(2,1)S(1)} %pad.4.refs_2_.refs_15_.kv_ref) | copy-start | bytes 491524
  12.9 21.7 %collective-permute-start = (bf16[128,640]{1,0:T(8,128)(2,1)S(1)}, bf16[128,640]{1,0:T(8,128)(2,1)S(1)}, u32[]{:S(2)}, u32[]{:S(2)}) collective-permute-start(bf16[128,640]{1,0:T(8,128)(2,1)S(1)} %pad.4.refs_2_.refs_15_.kv_ref), channel_id=1, source_target_pairs={{0,4},{1,5},{2,6},{3,7},{4,0},{5,1},{6,2},{7,3},{8,12},{9,13},{10,... | collective-permute-start | bytes 491528 | tf_op jit(solution)/shard_map/ppermute | solution.py:474
  34.6 6.4 %copy-start.5 = (bf16[128,640]{1,0:T(8,128)(2,1)}, bf16[128,640]{1,0:T(8,128)(2,1)S(1)}, u32[]{:S(2)}) copy-start(bf16[128,640]{1,0:T(8,128)(2,1)S(1)} %collective-permute-done.refs_3_.refs_16_) | copy-start | bytes 491524
  35.1 24.2 %collective-permute-start.1 = (bf16[128,2048]{1,0:T(8,128)(2,1)S(1)}, bf16[128,2048]{1,0:T(8,128)(2,1)S(1)}, u32[]{:S(2)}, u32[]{:S(2)}) collective-permute-start(bf16[128,2048]{1,0:T(8,128)(2,1)S(1)} %get-tuple-element.16), channel_id=1, source_target_pairs={{0,1},{1,2},{2,3},{3,0},{4,5},{5,6},{6,7},{7,4},{8,9},{9,10},{10,1... | collective-permute-start | bytes 1572872 | tf_op jit(solution)/shard_map/ppermute | solution.py:480
  36.3 22.9 %collective-permute-start.2 = (bf16[128,2048]{1,0:T(8,128)(2,1)S(1)}, bf16[128,2048]{1,0:T(8,128)(2,1)S(1)}, u32[]{:S(2)}, u32[]{:S(2)}) collective-permute-start(bf16[128,2048]{1,0:T(8,128)(2,1)S(1)} %get-tuple-element.19), channel_id=1, source_target_pairs={{0,3},{1,0},{2,1},{3,2},{4,7},{5,4},{6,5},{7,6},{8,11},{9,8},{10,9... | collective-permute-start | bytes 1572872 | tf_op jit(solution)/shard_map/ppermute | solution.py:480
  37.9 30.9 %collective-permute-start.6 = (bf16[128,2048]{1,0:T(8,128)(2,1)S(1)}, bf16[128,2048]{1,0:T(8,128)(2,1)S(1)}, u32[]{:S(2)}, u32[]{:S(2)}) collective-permute-start(bf16[128,2048]{1,0:T(8,128)(2,1)S(1)} %get-tuple-element.23), channel_id=1, source_target_pairs={{0,2},{1,3},{2,0},{3,1},{4,6},{5,7},{6,4},{7,5},{8,10},{9,11},{10,... | collective-permute-start | bytes 1572872 | tf_op jit(solution)/shard_map/ppermute | solution.py:480
  41.0 0.7 copy-start.9
  41.7 4.8 %collective-permute-start.3 = (bf16[128,768]{1,0:T(8,128)(2,1)S(1)}, bf16[128,768]{1,0:T(8,128)(2,1)S(1)}, u32[]{:S(2)}, u32[]{:S(2)}) collective-permute-start(bf16[128,768]{1,0:T(8,128)(2,1)S(1)} %get-tuple-element.20), channel_id=1, source_target_pairs={{0,4},{1,5},{2,6},{3,7},{4,0},{5,1},{6,2},{7,3},{8,12},{9,13},{10,... | collective-permute-start | bytes 589832 | tf_op jit(solution)/shard_map/ppermute | solution.py:480
  41.9 8.1 %collective-permute-start.4 = (bf16[128,768]{1,0:T(8,128)(2,1)S(1)}, bf16[128,768]{1,0:T(8,128)(2,1)S(1)}, u32[]{:S(2)}, u32[]{:S(2)}) collective-permute-start(bf16[128,768]{1,0:T(8,128)(2,1)S(1)} %get-tuple-element.21), channel_id=1, source_target_pairs={{0,5},{1,6},{2,7},{3,4},{4,1},{5,2},{6,3},{7,0},{8,13},{9,14},{10,... | collective-permute-start | bytes 589832 | tf_op jit(solution)/shard_map/ppermute | solution.py:480
  46.5 23.2 %copy-start.14 = (bf16[128,768]{1,0:T(8,128)(2,1)}, bf16[128,768]{1,0:T(8,128)(2,1)S(1)}, u32[]{:S(2)}) copy-start(bf16[128,768]{1,0:T(8,128)(2,1)S(1)} %collective-permute-done.3.refs_6_) | copy-start | bytes 589828
  46.5 7.8 %collective-permute-start.5 = (bf16[128,768]{1,0:T(8,128)(2,1)S(1)}, bf16[128,768]{1,0:T(8,128)(2,1)S(1)}, u32[]{:S(2)}, u32[]{:S(2)}) collective-permute-start(bf16[128,768]{1,0:T(8,128)(2,1)S(1)} %get-tuple-element.22), channel_id=1, source_target_pairs={{0,7},{1,4},{2,5},{3,6},{4,3},{5,0},{6,1},{7,2},{8,15},{9,12},{10,... | collective-permute-start | bytes 589832 | tf_op jit(solution)/shard_map/ppermute | solution.py:480
  50.0 19.6 %copy-start.15 = (bf16[128,768]{1,0:T(8,128)(2,1)}, bf16[128,768]{1,0:T(8,128)(2,1)S(1)}, u32[]{:S(2)}) copy-start(bf16[128,768]{1,0:T(8,128)(2,1)S(1)} %collective-permute-done.4.refs_7_) | copy-start | bytes 589828
  50.1 9.2 %collective-permute-start.7 = (bf16[128,768]{1,0:T(8,128)(2,1)S(1)}, bf16[128,768]{1,0:T(8,128)(2,1)S(1)}, u32[]{:S(2)}, u32[]{:S(2)}) collective-permute-start(bf16[128,768]{1,0:T(8,128)(2,1)S(1)} %get-tuple-element.24), channel_id=1, source_target_pairs={{0,6},{1,7},{2,4},{3,5},{4,2},{5,3},{6,0},{7,1},{8,14},{9,15},{10,... | collective-permute-start | bytes 589832 | tf_op jit(solution)/shard_map/ppermute | solution.py:480
  54.3 15.4 %copy-start.16 = (bf16[128,768]{1,0:T(8,128)(2,1)}, bf16[128,768]{1,0:T(8,128)(2,1)S(1)}, u32[]{:S(2)}) copy-start(bf16[128,768]{1,0:T(8,128)(2,1)S(1)} %collective-permute-done.5.refs_8_) | copy-start | bytes 589828
  59.2 10.4 %copy-start.17 = (bf16[128,768]{1,0:T(8,128)(2,1)}, bf16[128,768]{1,0:T(8,128)(2,1)S(1)}, u32[]{:S(2)}) copy-start(bf16[128,768]{1,0:T(8,128)(2,1)S(1)} %collective-permute-done.7.refs_10_) | copy-start | bytes 589828
  59.2 10.4 %copy-start.11 = (bf16[128,2048]{1,0:T(8,128)(2,1)}, bf16[128,2048]{1,0:T(8,128)(2,1)S(1)}, u32[]{:S(2)}) copy-start(bf16[128,2048]{1,0:T(8,128)(2,1)S(1)} %collective-permute-done.1.refs_4_) | copy-start | bytes 1572868
  59.2 9.6 %copy-start.12 = (bf16[128,2048]{1,0:T(8,128)(2,1)}, bf16[128,2048]{1,0:T(8,128)(2,1)S(1)}, u32[]{:S(2)}) copy-start(bf16[128,2048]{1,0:T(8,128)(2,1)S(1)} %collective-permute-done.2.refs_5_) | copy-start | bytes 1572868
  68.8 0.8 copy-start.13
  83.3 15.9 %all-to-all-start.2 = ((bf16[8,128,512]{2,1,0:T(8,128)(2,1)}), bf16[8,128,512]{2,1,0:T(8,128)(2,1)S(1)}, u32[]{:S(2)}, u32[]{:S(2)}) async-start(bf16[8,128,512]{2,1,0:T(8,128)(2,1)} %bitcast.18), calls=%async_computation.2 | async-start | bytes 2097152 | tf_op jit(solution)/shard_map/all_to_all | solution.py:466
  99.1 5.6 %copy-start.4 = (bf16[128,640]{1,0:T(8,128)(2,1)S(1)}, bf16[128,640]{1,0:T(8,128)(2,1)}, u32[]{:S(2)}) copy-start(bf16[128,640]{1,0:T(8,128)(2,1)} %copy-done.3) | copy-start | bytes 491524
  99.1 5.6 %copy-start.7 = (f32[512]{0:T(512)S(1)}, f32[512]{0:T(512)}, u32[]{:S(2)}) copy-start(f32[512]{0:T(512)} %param.10) | copy-start | bytes 6148
  99.1 5.6 %copy-start.8 = (s32[1,16]{1,0:T(1,128)S(1)}, s32[1,16]{1,0:T(1,128)}, u32[]{:S(2)}) copy-start(s32[1,16]{1,0:T(1,128)} %param.14) | copy-start | bytes 196
  99.1 28.2 %copy-start.6 = (s32[32,2]{0,1:T(2,128)S(1)}, s32[32,2]{0,1:T(2,128)}, u32[]{:S(2)}) copy-start(s32[32,2]{0,1:T(2,128)} %param.15) | copy-start | bytes 772
  99.1 56.6 %all-to-all-start.1 = ((bf16[8,128,512]{2,1,0:T(8,128)(2,1)}), bf16[8,128,512]{2,1,0:T(8,128)(2,1)S(1)}, u32[]{:S(2)}, u32[]{:S(2)}) async-start(bf16[8,128,512]{2,1,0:T(8,128)(2,1)} %bitcast.17), calls=%async_computation.1 | async-start | bytes 2097152 | tf_op jit(solution)/shard_map/all_to_all | solution.py:466
  105.7 4.7 %collective-permute-start.8 = (bf16[2,288,128]{2,1,0:T(8,128)(2,1)S(1)}, bf16[2,288,128]{2,1,0:T(8,128)(2,1)S(1)}, u32[]{:S(2)}, u32[]{:S(2)}) collective-permute-start(bf16[2,288,128]{2,1,0:T(8,128)(2,1)S(1)} %pages.1.one_ref), channel_id=1, source_target_pairs={{0,8},{8,0},{16,24},{24,16},{32,40},{40,32},{48,56},{56,48},{64,72... | collective-permute-start | bytes 442376 | tf_op jit(solution)/shard_map/ppermute | solution.py:455
  110.5 9.8 %collective-permute-start.10 = (bf16[4,288,128]{2,1,0:T(8,128)(2,1)S(1)}, bf16[4,288,128]{2,1,0:T(8,128)(2,1)S(1)}, u32[]{:S(2)}, u32[]{:S(2)}) collective-permute-start(bf16[4,288,128]{2,1,0:T(8,128)(2,1)S(1)} %merge.1.refs_0_), channel_id=1, source_target_pairs={{0,128},{8,136},{16,144},{24,152},{32,160},{40,168},{48,176},{56,1... | collective-permute-start | bytes 884744 | tf_op jit(solution)/shard_map/ppermute | solution.py:459
  113.4 13.4 %collective-permute-start.11 = (bf16[4,288,128]{2,1,0:T(8,128)(2,1)S(1)}, bf16[4,288,128]{2,1,0:T(8,128)(2,1)S(1)}, u32[]{:S(2)}, u32[]{:S(2)}) collective-permute-start(bf16[4,288,128]{2,1,0:T(8,128)(2,1)S(1)} %merge.1.refs_0_), channel_id=1, source_target_pairs={{0,192},{8,200},{16,208},{24,216},{32,224},{40,232},{48,240},{56,2... | collective-permute-start | bytes 884744 | tf_op jit(solution)/shard_map/ppermute | solution.py:459
  114.3 13.0 %collective-permute-start.9 = (bf16[4,288,128]{2,1,0:T(8,128)(2,1)S(1)}, bf16[4,288,128]{2,1,0:T(8,128)(2,1)S(1)}, u32[]{:S(2)}, u32[]{:S(2)}) collective-permute-start(bf16[4,288,128]{2,1,0:T(8,128)(2,1)S(1)} %merge.1.refs_0_), channel_id=1, source_target_pairs={{0,64},{8,72},{16,80},{24,88},{32,96},{40,104},{48,112},{56,120},{... | collective-permute-start | bytes 884744 | tf_op jit(solution)/shard_map/ppermute | solution.py:459
  130.6 9.8 %collective-permute-start.12 = (bf16[2,288,128]{2,1,0:T(8,128)(2,1)S(1)}, bf16[2,288,128]{2,1,0:T(8,128)(2,1)S(1)}, u32[]{:S(2)}, u32[]{:S(2)}) collective-permute-start(bf16[2,288,128]{2,1,0:T(8,128)(2,1)S(1)} %get-tuple-element.32), channel_id=1, source_target_pairs={{0,16},{8,24},{16,32},{24,40},{32,48},{40,56},{48,0},{56,8},{64,80... | collective-permute-start | bytes 442376 | tf_op jit(solution)/shard_map/ppermute | solution.py:461
  133.8 11.8 %collective-permute-start.13 = (bf16[2,288,128]{2,1,0:T(8,128)(2,1)S(1)}, bf16[2,288,128]{2,1,0:T(8,128)(2,1)S(1)}, u32[]{:S(2)}, u32[]{:S(2)}) collective-permute-start(bf16[2,288,128]{2,1,0:T(8,128)(2,1)S(1)} %get-tuple-element.31), channel_id=1, source_target_pairs={{0,32},{8,40},{16,48},{24,56},{32,0},{40,8},{48,16},{56,24},{64,96... | collective-permute-start | bytes 442376 | tf_op jit(solution)/shard_map/ppermute | solution.py:461
  138.0 15.4 %collective-permute-start.14 = (bf16[2,288,128]{2,1,0:T(8,128)(2,1)S(1)}, bf16[2,288,128]{2,1,0:T(8,128)(2,1)S(1)}, u32[]{:S(2)}, u32[]{:S(2)}) collective-permute-start(bf16[2,288,128]{2,1,0:T(8,128)(2,1)S(1)} %get-tuple-element.30), channel_id=1, source_target_pairs={{0,48},{8,56},{16,0},{24,8},{32,16},{40,24},{48,32},{56,40},{64,11... | collective-permute-start | bytes 442376 | tf_op jit(solution)/shard_map/ppermute | solution.py:461

commit v2 on v1

v2 whole, which is shorter than its diff:
```python
import functools
import math

import jax
import jax.numpy as jnp
from jax import lax
from jax.experimental import pallas as pl
from jax.experimental.pallas import tpu as pltpu
from jax.sharding import PartitionSpec as P


HEADS = 64
HD = 128
ROPE = 64
LAT = 512
QW = HD + ROPE
PAIR = 2 * QW
BLK = 64
TILE = 256
GROUPS = 8
LOCAL = 2 * BLK
KVP = LAT + 128
PAGE = BLK * (LAT + ROPE) // 128

CHUNKS = 2
PAIRS = 4 // CHUNKS
QPART = PAIRS * PAIR
OPART = PAIRS * 2 * HD

theta_base = 10000.0
epsilon = 1e-06
masked_fill = -1e30
log2_scale = math.log2(math.e) * QW ** (-0.5)


NT = (((1,), (1,)), ((), ()))
SMEM = pl.BlockSpec(memory_space=pltpu.SMEM)
VMEM = pl.BlockSpec(memory_space=pltpu.VMEM)
ANY = pl.BlockSpec(memory_space=pl.ANY)

OFFSETS = ((0, 0), (0, 1), (0, 3), (1, 0), (1, 1), (1, 3), (0, 2), (1, 2))
BESIDE = {1: 4, 2: 5, 6: 7}
EARLY, LATE = (7, 4, 5, 3), (6, 1, 2)


def partner(context, k, back=False):
    dz, dy = OFFSETS[k]
    z, y = context // 4, context % 4
    step = 4 - dy if back else dy
    return ((z + dz) % 2) * 4 + (y + step) % 4


def forward(k):
    return [(d, partner(d, k)) for d in range(GROUPS)]


def params(limit):
    return pltpu.CompilerParams(vmem_limit_bytes=limit << 20)


def rotate_lanes(x, cosine, sine, lane):
    half = ROPE // 2
    swapped = jnp.where(lane % ROPE < half, pltpu.roll(x, 128 - half, 1), pltpu.roll(x, half, 1))
    return x * cosine + swapped * sine


def pack_kernel(chunk, partners, n_kv, *refs):
    ctx_ref, q_ref, *refs = refs
    kvs, refs = refs[:n_kv], refs[n_kv:]
    outs, (held, sems) = refs[: len(partners)], refs[len(partners) :]
    loads, stores = [], []
    for n, k in enumerate(partners):
        column = partner(ctx_ref[0], k) * (4 * PAIR) + chunk * QPART
        columns = pl.ds(pl.multiple_of(column, 128), QPART)
        loads.append(pltpu.make_async_copy(q_ref.at[0, :, columns], held.at[n], sems.at[0, n]))
        loads[-1].start()
    for n in range(len(partners)):
        for i, kv in enumerate(kvs):
            columns = pl.ds(QPART + i * KVP, KVP)
            stores.append(pltpu.make_async_copy(kv, outs[n].at[:, columns], sems.at[2 + i, n]))
            stores[-1].start()
    for n in range(len(partners)):
        loads[n].wait()
        stores.append(pltpu.make_async_copy(held.at[n], outs[n].at[:, :QPART], sems.at[1, n]))
        stores[-1].start()
    for store in stores:
        store.wait()


def pack(context, q_heads, chunk, partners, kvs=()):
    count = len(partners)
    outs = pl.pallas_call(
        functools.partial(pack_kernel, chunk, partners, len(kvs)),
        in_specs=[SMEM, ANY] + [VMEM] * len(kvs),
        out_specs=[ANY] * count,
        out_shape=[jax.ShapeDtypeStruct((LOCAL, QPART + len(kvs) * KVP), jnp.bfloat16)] * count,
        scratch_shapes=[
            pltpu.VMEM((count, LOCAL, QPART), jnp.bfloat16),
            pltpu.SemaphoreType.DMA((4, count)),
        ],
        compiler_params=params(8 if kvs else 60),
        name="pack",
    )(context, q_heads, *kvs)
    return dict(zip(partners, outs))


def pack_all_kernel(chunk, q_ref, o_ref, held, sems):
    loads, stores = [], []
    for j in range(GROUPS):
        columns = pl.ds(j * (4 * PAIR) + chunk * QPART, QPART)
        loads.append(pltpu.make_async_copy(q_ref.at[0, :, columns], held.at[j], sems.at[0, j]))
        loads[-1].start()
    for j in range(GROUPS):
        loads[j].wait()
        stores.append(pltpu.make_async_copy(held.at[j], o_ref.at[j], sems.at[1, j]))
        stores[-1].start()
    for store in stores:
        store.wait()


def pack_all(chunk, q_heads):
    shape = (GROUPS, LOCAL, QPART)
    return pl.pallas_call(
        functools.partial(pack_all_kernel, chunk),
        in_specs=[ANY],
        out_specs=ANY,
        out_shape=jax.ShapeDtypeStruct(shape, jnp.bfloat16),
        scratch_shapes=[pltpu.VMEM(shape, jnp.bfloat16), pltpu.SemaphoreType.DMA((2, GROUPS))],
        compiler_params=params(60),
        name="pack_all",
    )(q_heads)


def attend_kernel(chunk, *refs):
    first = chunk == 0
    ctx_ref, order_ref, length_ref, *refs = refs
    if first:
        arrived, refs = refs[:GROUPS], refs[GROUPS:]
        w_hbm, cos_hbm, sin_hbm, gain_ref, kv_hbm, kvz_hbm, o_ref, cs_hbm, krl_hbm, krr_hbm, *refs = refs
    else:
        stacked, w_hbm, cos_hbm, sin_hbm, cs_hbm, krl_hbm, krr_hbm, o_ref, *refs = refs
        arrived = [stacked.at[k] for k in range(GROUPS)]
    w_ref, cs, krl, krr, cos_ref, sin_ref, qs, os, k0, k1, v, sems, out_sems = refs
    total = cs.shape[0]
    context = ctx_ref[0]
    started = []

    def load(source, target):
        copy = pltpu.make_async_copy(source, target, sems.at[len(started)])
        copy.start()
        started.append(copy)
        return copy

    rows_of = {}
    if first:
        rows_of = {0: (kv_hbm, 0), 3: (kvz_hbm, 0)}
        for k, beyond in BESIDE.items():
            rows_of[k] = (arrived[k], QPART)
            rows_of[beyond] = (arrived[k], QPART + KVP)
    places, moves = [], []
    for k in range(GROUPS):
        source = partner(context, k, back=True) if first else k
        for i in range(2):
            place = pl.multiple_of(order_ref[2 * source + i] * BLK, BLK)
            places.append((2 * source + i, place))
            moves.append((k, pl.ds(i * BLK, BLK), pl.ds(place, BLK)))
    keys_here = []
    if first:
        for k, here, there in moves:
            ref, at = rows_of[k]
            keys_here.append(load(ref.at[here, pl.ds(at, LAT)], cs.at[there]))
            keys_here.append(load(ref.at[here, pl.ds(at + LAT, KVP - LAT)], krl.at[there]))
    else:
        keys_here = [load(cs_hbm, cs), load(krl_hbm, krl), load(krr_hbm, krr)]
    tables_here = [load(cos_hbm, cos_ref), load(sin_hbm, sin_ref)]
    weights_here, queries_here = [], []
    for pair in range(PAIRS):
        heads = pl.ds(2 * (chunk * PAIRS + pair), 2)
        weights_here.append(load(w_hbm.at[heads], w_ref.at[pl.ds(2 * pair, 2)]))
        queries_here.append(
            [load(arrived[k].at[here, pl.ds(pair * PAIR, PAIR)], qs.at[pair, there]) for k, here, there in moves]
        )
    for copy in keys_here + tables_here * first:
        copy.wait()

    lane = lax.broadcasted_iota(jnp.int32, (TILE, 128), 1)
    if first:
        for t in range(total // TILE):
            rows = slice(t * TILE, (t + 1) * TILE)
            latent = cs[rows, :].astype(jnp.float32)
            mean_square = jnp.mean(latent * latent, axis=-1, keepdims=True)
            cs[rows, :] = (latent * lax.rsqrt(mean_square + epsilon) * gain_ref[...]).astype(jnp.bfloat16)
            turned = rotate_lanes(krl[rows, :].astype(jnp.float32), cos_ref[rows, :], sin_ref[rows, :], lane)
            krl[rows, :] = turned.astype(jnp.bfloat16)
            krr[rows, :] = pltpu.roll(turned, ROPE, 1).astype(jnp.bfloat16)
    kept = [load(cs, cs_hbm), load(krl, krl_hbm), load(krr, krr_hbm)] if first else []
    length = length_ref[0]

    row = lax.broadcasted_iota(jnp.int32, (TILE, TILE), 0)
    column = lax.broadcasted_iota(jnp.int32, (TILE, TILE), 1)
    stores = []

    def project(pair):
        gap = jnp.zeros((ROPE, LAT), jnp.bfloat16)
        w0, w1 = w_ref[2 * pair], w_ref[2 * pair + 1]
        wk = jnp.concatenate([w0[:HD], gap, w1[:HD], gap], axis=0)
        wv = jnp.concatenate([w0[HD:], w1[HD:]], axis=0)
        for t in range(total // TILE):
            rows = slice(t * TILE, (t + 1) * TILE)
            cache = cs[rows, :]
            kn = lax.dot_general(cache, wk, NT, preferred_element_type=jnp.float32).astype(jnp.bfloat16)
            k0[pair, rows, :128] = kn[:, :128]
            k0[pair, rows, 128:] = krl[rows, :]
            k1[pair, rows, :128] = kn[:, 128:256]
            k1[pair, rows, 128:] = kn[:, 256:] + krr[rows, :]
            v[pair, rows, :] = lax.dot_general(cache, wv, NT, preferred_element_type=jnp.float32).astype(jnp.bfloat16)

    def score(pair, t, head):
        rows = slice(t * TILE, (t + 1) * TILE)
        cosine, sine = cos_ref[rows, :], sin_ref[rows, :]
        mixed = qs[pair, rows, 128 * (1 + head) : 128 * (2 + head)].astype(jnp.float32)
        turned = rotate_lanes(mixed, cosine, sine, lane)
        if head == 0:
            mixed = jnp.where(lane < ROPE, turned, mixed).astype(jnp.bfloat16)
            query = jnp.concatenate([qs[pair, rows, :128], mixed], axis=1)
        else:
            mixed = jnp.where(lane < ROPE, mixed, turned).astype(jnp.bfloat16)
            query = jnp.concatenate([qs[pair, rows, 128:256], mixed], axis=1)
        k = (k0, k1)[head]
        last = lax.dot_general(query, k[pair, rows, :], NT, preferred_element_type=jnp.float32)
        last = jnp.where(column <= row, last, masked_fill)
        if t == 0:
            return [last]
        return [lax.dot_general(query, k[pair, : t * TILE, :], NT, preferred_element_type=jnp.float32), last]

    def weigh(pair, t, head, scores):
        rows = slice(t * TILE, (t + 1) * TILE)
        side = slice(head * HD, (head + 1) * HD)
        valid = lax.broadcasted_iota(jnp.int32, (TILE, HD), 0) + t * TILE < length
        top = functools.reduce(jnp.maximum, [jnp.max(s, axis=1, keepdims=True) for s in scores])
        parts = [jnp.exp2((s - top) * log2_scale) for s in scores]
        bottom = functools.reduce(jnp.add, [jnp.sum(p, axis=1, keepdims=True) for p in parts])
        values = [v[pair, : t * TILE, side], v[pair, rows, side]][-len(parts) :]
        o = functools.reduce(
            jnp.add,
            [jnp.dot(p.astype(jnp.bfloat16), u, preferred_element_type=jnp.float32) for p, u in zip(parts, values)],
        )
        os[pair, rows, side] = jnp.where(valid, o / bottom, 0.0).astype(jnp.bfloat16)

    for pair in range(PAIRS):
        weights_here[pair].wait()
        project(pair)
        for copy in queries_here[pair] + tables_here * (not first and pair == 0):
            copy.wait()
        items = [(t, head) for t in range(total // TILE) for head in range(2)]
        ahead = score(pair, *items[0])
        for n, item in enumerate(items):
            scores = ahead
            if n + 1 < len(items):
                ahead = score(pair, *items[n + 1])
            weigh(pair, *item, scores)
        for n, (block, place) in enumerate(places):
            columns = pl.ds(pair * (2 * HD), 2 * HD)
            stores.append(
                pltpu.make_async_copy(
                    os.at[pair, pl.ds(place, BLK)], o_ref.at[block, :, columns], out_sems.at[pair, n]
                )
            )
            stores[-1].start()
    for copy in stores + kept:
        copy.wait()


def attend(chunk, context, order_row, length, arrived, kv_up, extra):
    first = chunk == 0
    total = GROUPS * LOCAL
    shapes = [(2 * GROUPS, BLK, OPART)] + [(total, LAT), (total, 128), (total, 128)] * first
    n_arrived = len(arrived)
    sides = [ANY, ANY, VMEM, ANY, ANY] if first else [ANY] * 5
    outs = pl.pallas_call(
        functools.partial(attend_kernel, chunk),
        in_specs=[SMEM, SMEM, SMEM] + [ANY] * (n_arrived + 1) + sides,
        out_specs=[ANY] * len(shapes),
        out_shape=[jax.ShapeDtypeStruct(shape, jnp.bfloat16) for shape in shapes],
        scratch_shapes=[
            pltpu.VMEM((2 * PAIRS, 2 * HD, LAT), jnp.bfloat16),
            pltpu.VMEM((total, LAT), jnp.bfloat16),
            pltpu.VMEM((total, 128), jnp.bfloat16),
            pltpu.VMEM((total, 128), jnp.bfloat16),
            pltpu.VMEM((total, 128), jnp.float32),
            pltpu.VMEM((total, 128), jnp.float32),
            pltpu.VMEM((PAIRS, total, PAIR), jnp.bfloat16),
            pltpu.VMEM((PAIRS, total, 2 * HD), jnp.bfloat16),
            pltpu.VMEM((PAIRS, total, 256), jnp.bfloat16),
            pltpu.VMEM((PAIRS, total, 256), jnp.bfloat16),
            pltpu.VMEM((PAIRS, total, 256), jnp.bfloat16),
            pltpu.SemaphoreType.DMA((7 + (2 + PAIRS) * 2 * GROUPS,)),
            pltpu.SemaphoreType.DMA((PAIRS, 2 * GROUPS)),
        ],
        compiler_params=params(60),
        cost_estimate=pl.CostEstimate(
            flops=PAIRS * 2_200_000_000, bytes_accessed=6_000_000, transcendentals=PAIRS * 1_300_000
        ),
        name="attend",
    )(context, order_row, length, *arrived, kv_up, *extra)
    return outs[0].reshape(GROUPS, LOCAL, OPART), outs[1:]


def unpack_kernel(chunk, part_ref, *refs):
    o_ref, sems = refs[-2:]
    stores = []
    for j in range(GROUPS):
        columns = pl.ds(j * (8 * HD) + chunk * OPART, OPART)
        stores.append(pltpu.make_async_copy(part_ref.at[j], o_ref.at[0, :, columns], sems.at[j]))
        stores[-1].start()
    for store in stores:
        store.wait()


def unpack(chunk, part, out):
    more = [] if out is None else [out]
    return pl.pallas_call(
        functools.partial(unpack_kernel, chunk),
        in_specs=[VMEM] + [ANY] * len(more),
        out_specs=ANY,
        out_shape=jax.ShapeDtypeStruct((1, LOCAL, HEADS * HD), jnp.bfloat16),
        scratch_shapes=[pltpu.SemaphoreType.DMA((GROUPS,))],
        input_output_aliases={1: 0} if more else {},
        compiler_params=params(8),
        name="unpack",
    )(part, *more)


def pages_kernel(ctx_ref, order_ref, offset_ref, kv_ref, gain_ref, freq_ref, o_ref, rows, page):
    row = lax.broadcasted_iota(jnp.int32, (LOCAL, 128), 0)
    lane = lax.broadcasted_iota(jnp.int32, (LOCAL, 128), 1)
    first, second = order_ref[2 * ctx_ref[0]], order_ref[2 * ctx_ref[0] + 1]
    position = jnp.where(row < BLK, first, second) * BLK + row % BLK + offset_ref[0]
    angles = position.astype(jnp.float32) * freq_ref[...]
    sine = jnp.sin(angles)
    latent = kv_ref[:, :LAT].astype(jnp.float32)
    mean_square = jnp.mean(latent * latent, axis=-1, keepdims=True)
    normed = latent * lax.rsqrt(mean_square + epsilon) * gain_ref[...]
    for t in range(4):
        rows[t] = normed[:, 128 * t : 128 * (t + 1)].astype(jnp.bfloat16).astype(jnp.float32)
    rope = kv_ref[:, LAT:].astype(jnp.float32)
    rope = rotate_lanes(rope, jnp.cos(angles), jnp.where(lane % ROPE < ROPE // 2, -sine, sine), lane)
    rows[4] = rope.astype(jnp.bfloat16).astype(jnp.float32)
    half = BLK // 2
    left = lax.broadcasted_iota(jnp.int32, (half, 128), 1) < ROPE
    for i in range(2):
        even = [rows[t, pl.ds(i * BLK, half, stride=2), :] for t in range(5)]
        odd = [pltpu.roll(rows[t, pl.ds(i * BLK + 1, half, stride=2), :], ROPE, 1) for t in range(5)]
        for t in range(9):
            if t < 4:
                tile = even[t]
            elif t == 4:
                tile = jnp.where(left, even[4], odd[0])
            else:
                tile = jnp.where(left, odd[t - 5], odd[t - 4])
            page[pl.ds(t, half, stride=9), :] = tile
        o_ref[i] = page[...].astype(jnp.bfloat16)


def make_pages(context, order_row, offsets, kv, gain):
    half = ROPE // 2
    lane = jnp.arange(128) % half
    freq = jnp.exp(-math.log(theta_base) * lane.astype(jnp.float32) / half)
    return pl.pallas_call(
        pages_kernel,
        in_specs=[SMEM] * 3 + [VMEM] * 3,
        out_specs=VMEM,
        out_shape=jax.ShapeDtypeStruct((2, PAGE, 128), jnp.bfloat16),
        scratch_shapes=[pltpu.VMEM((5, LOCAL, 128), jnp.float32), pltpu.VMEM((PAGE, 128), jnp.float32)],
        compiler_params=params(8),
        name="pages",
    )(context, order_row, offsets, kv, gain, freq[None])


def relay_kernel(req_ref, owners_ref, *refs):
    parts, outs, (table, count, sems) = refs[:4], refs[4:8], refs[8:]
    me = req_ref[0]
    my_x, my_z, my_core = me // 8, (me // 2) % 4, me % 2
    for i in range(16):
        table[i] = -1
    for i in range(8):
        count[i] = 0
    for z in range(4):
        for page in range(2):
            owner = owners_ref[page, request(my_x, z, my_core)]

            @pl.when((owner // 2) % 4 == my_z)
            def _():
                where = 2 * ((owner // 8 + 4 - my_x) % 4) + ((owner % 2) ^ my_core)
                slot = count[where]
                table[2 * where + jnp.minimum(slot, 1)] = 2 * ((my_z + 4 - z) % 4) + page
                count[where] = slot + 1

    def move(i, d):
        return pltpu.make_async_copy(parts[d].at[jnp.maximum(table[i], 0) % 2], outs[i // 4].at[i % 4], sems.at[i])

    for i in range(16):
        for d in range(4):

            @pl.when((table[i] >= 0) & (table[i] // 2 == d))
            def _():
                move(i, d).start()

    for i in range(16):

        @pl.when(table[i] >= 0)
        def _():
            move(i, 0).wait()


def relay_pages(req, owners, parts):
    page = parts[0].shape[1:]
    return pl.pallas_call(
        relay_kernel,
        in_specs=[SMEM, SMEM] + [ANY] * 4,
        out_specs=[VMEM] * 4,
        out_shape=[jax.ShapeDtypeStruct((4,) + page, parts[0].dtype)] * 4,
        scratch_shapes=[
            pltpu.SMEM((16,), jnp.int32),
            pltpu.SMEM((8,), jnp.int32),
            pltpu.SemaphoreType.DMA((16,)),
        ],
        compiler_params=params(8),
        name="relay_pages",
    )(req, owners, *parts)


def find(owner, target, my_x):
    flat = 2 * lax.broadcasted_iota(jnp.int32, owner.shape, 1) + lax.broadcasted_iota(jnp.int32, owner.shape, 0)
    last = jnp.max(jnp.where(owner == target, flat, 0))
    first = jnp.minimum(jnp.min(jnp.where(owner == target, flat, 4 * owner.shape[1])), last)
    found = []
    for page in (first, last):
        source = page // 2
        found.append(((my_x + 4 - source // 8) % 4, source % 2))
    same = (found[0][0] == found[1][0]) & (found[0][1] == found[1][1])
    return [found[0] + (0,), found[1] + (jnp.where(same, 1, 0),)]


def cross_kernel(req_ref, owners_ref, *refs):
    parts, o_ref = refs[:4], refs[4]
    me = req_ref[0]
    for i, (turn, core, slot) in enumerate(find(owners_ref[...], me ^ 1, me // 8)):
        for d, part in enumerate(parts):

            @pl.when((core == me % 2) & (turn == d))
            def _():
                o_ref[i] = part[2 + slot]


def keep_kernel(req_ref, owners_ref, crossed_ref, *refs):
    parts, o_ref = refs[:4], refs[4]
    me = req_ref[0]
    for i, (turn, core, slot) in enumerate(find(owners_ref[...], me, me // 8)):
        for d, part in enumerate(parts):

            @pl.when((core == me % 2) & (turn == d))
            def _():
                o_ref[i] = part[slot]

        @pl.when(core != me % 2)
        def _():
            o_ref[i] = crossed_ref[i]


def choose(kernel, req, owners, parts):
    return pl.pallas_call(
        kernel,
        in_specs=[SMEM] + [VMEM] * (1 + len(parts)),
        out_specs=VMEM,
        out_shape=jax.ShapeDtypeStruct((2,) + parts[0].shape[1:], parts[0].dtype),
        compiler_params=params(8),
    )(req, owners, *parts)


def request(x, z, core):
    return (x * 4 + z) * 2 + core


EACH = [(x, z, c) for x in range(4) for z in range(4) for c in range(2)]


def along_x(d):
    return [(request(x, z, c), request((x + d) % 4, z, c)) for x, z, c in EACH]


def along_z(d):
    return [(request(x, z, c), request(x, (z + d) % 4, c)) for x, z, c in EACH]


def ship(pages, owners):
    req, owners = lax.axis_index("req").reshape(1), owners.T
    parts = [pages] + [lax.ppermute(pages, "req", along_z(d)) for d in (1, 2, 3)]
    outgoing = relay_pages(req, owners, parts)
    parts = [outgoing[0]] + [lax.ppermute(outgoing[d], "req", along_x(d)) for d in (1, 2, 3)]
    crossing = choose(cross_kernel, req, owners, parts)
    crossed = lax.ppermute(crossing, "req", [(request(x, z, c), request(x, z, 1 - c)) for x, z, c in EACH])
    return choose(keep_kernel, req, owners, [crossed] + parts)


def exchange(array):
    return lax.all_to_all(array, "ctx", split_axis=0, concat_axis=0, tiled=True)


def body(q_heads, kv_latent, latent_gain, kv_up, offsets, lengths, block_order, owners):
    context = lax.axis_index("ctx").reshape(1)
    order_row = block_order[0]
    gain = latent_gain[None]
    padded = jnp.pad(kv_latent[0], ((0, 0), (0, KVP - kv_latent.shape[2])))
    beyond = lax.ppermute(padded, "ctx", forward(3))

    sent = pack(context, q_heads, 0, (0,) + EARLY)
    pages = make_pages(context, order_row, offsets, padded, gain)
    shipped = ship(pages, owners).reshape(1, 2, PAGE * 128)
    sent.update(pack(context, q_heads, 0, LATE, (padded, beyond)))
    arrived = [[sent[0]] + [lax.ppermute(sent[k], "ctx", forward(k)) for k in range(1, GROUPS)]]
    for chunk in range(1, CHUNKS):
        arrived.append([exchange(pack_all(chunk, q_heads))])
    offsets, _ = lax.optimization_barrier((offsets, sent[1]))
    lane = jnp.arange(128, dtype=jnp.int32)
    half = ROPE // 2
    frequency = jnp.exp(-math.log(theta_base) * (lane % half).astype(jnp.float32) / half)
    positions = offsets[0] + jnp.arange(GROUPS * LOCAL, dtype=jnp.int32)
    angles = positions.astype(jnp.float32)[:, None] * frequency[None, :]
    sign = jnp.where(lane % ROPE < half, -1.0, 1.0)
    extra = [jnp.cos(angles), jnp.sin(angles) * sign[None, :], gain, padded, beyond]
    attn_out = None
    for chunk in range(CHUNKS):
        out, kept = attend(chunk, context, order_row, lengths, arrived[chunk], kv_up, extra)
        extra = extra[:2] + list(kept) if chunk == 0 else extra
        attn_out = unpack(chunk, exchange(out), attn_out)
    return attn_out, shipped


def solution(mesh):
    in_specs = (
        P("req", "ctx", None),
        P("req", "ctx", None),
        P(),
        P("ctx", None, None),
        P("req"),
        P("req"),
        P("req", None),
        P(None, "ctx"),
    )
    out_specs = (P("req", "ctx", None), P("req", "ctx", None))
    return jax.shard_map(body, mesh=mesh, in_specs=in_specs, out_specs=out_specs, check_vma=False)
```

time: 157 us -> 154 us (0.981)
  the two profiles are of different devices: /device:TPU:1 before, /device:TPU:70 now
where the time goes in v2:
time: 154 us; the launch traced here: 151 us
  waiting for transfers between devices  69.2 us (45%)
  starting transfers between devices  39.1 us (25%)
  Pallas kernels  35.6 us (23%)
  other arithmetic  3.1 us (2%)
  between operations  2.4 us (2%)
  local copies, waits for them, and re-layouts  1.73 us (1%)
    pallas_call x2, Pallas kernels, attend(): pl.pallas_call(functools.partial(attend_kernel, chunk), in_specs=[SMEM, S...  24.2 us
    ppermute x1, waiting for transfers between devices, body(): beyond = lax.ppermute(padded, 'ctx', forward(3))  20.5 us
    ppermute x3, waiting for transfers between devices, ship(): lax.ppermute(pages, 'req', along_z(d))  18.4 us
    ppermute x7, waiting for transfers between devices, body(): lax.ppermute(sent[k], 'ctx', forward(k))  17.4 us
    all_to_all x3, starting transfers between devices, exchange(): return lax.all_to_all(array, 'ctx', split_axis=0, concat_axis=0, tiled=True)  14.3 us
    ppermute x7, starting transfers between devices, body(): lax.ppermute(sent[k], 'ctx', forward(k))  10.9 us
    ppermute x3, waiting for transfers between devices, ship(): lax.ppermute(outgoing[d], 'req', along_x(d))  10.4 us
    ppermute x3, starting transfers between devices, ship(): lax.ppermute(pages, 'req', along_z(d))  8.69 us
  transfers between devices with their start and end apart: 18, of which 13 were waited for; matrix products, arithmetic and copies ran while one was open for 3% of the time, Pallas kernels for 21%

profile of v2, /device:TPU:70, one launch (start us, length us, event | category | flops | bytes accessed | tf_op | source)
XLA Modules:
  0.0 151.2 jit_solution(10057581942706694411)
XLA Ops:
  0.6 2.3 %pack_all.1 = bf16[8,128,768]{2,1,0:T(8,128)(2,1)} custom-call(bf16[1,128,12288]{2,1,0:T(8,128)(2,1)} %refs_1_.3), custom_call_target="tpu_custom_call" | custom-call | tf_op jit(solution)/shard_map/pack_all/pallas_call | solution.py:123
  3.0 0.0 copy-start
  3.0 6.1 %all-to-all-start = ((bf16[8,128,768]{2,1,0:T(8,128)(2,1)}), bf16[8,128,768]{2,1,0:T(8,128)(2,1)}, u32[]{:S(2)}, u32[]{:S(2)}) async-start(bf16[8,128,768]{2,1,0:T(8,128)(2,1)} %pack_all.1), calls=%async_computation | async-start | bytes 3145728 | tf_op jit(solution)/shard_map/all_to_all | solution.py:507
  9.1 0.0 copy-done.7
  9.1 0.2 copy.11
  9.3 0.0 copy-start.1
  9.3 2.1 %collective-permute-start = (bf16[128,640]{1,0:T(8,128)(2,1)S(1)}, bf16[128,640]{1,0:T(8,128)(2,1)S(1)}, u32[]{:S(2)}, u32[]{:S(2)}) collective-permute-start(bf16[128,640]{1,0:T(8,128)(2,1)S(1)} %pad.4.refs_2_.refs_15_.kv_ref), channel_id=1, source_target_pairs={{0,4},{1,5},{2,6},{3,7},{4,0},{5,1},{6,2},{7,3},{8,12},{9,13},{10,... | collective-permute-start | bytes 491528 | tf_op jit(solution)/shard_map/ppermute | solution.py:515
  11.4 20.5 %collective-permute-done.refs_3_.refs_16_ = bf16[128,640]{1,0:T(8,128)(2,1)S(1)} collective-permute-done((bf16[128,640]{1,0:T(8,128)(2,1)S(1)}, bf16[128,640]{1,0:T(8,128)(2,1)S(1)}, u32[]{:S(2)}, u32[]{:S(2)}) %collective-permute-start) | collective-permute-done | bytes 163872 | tf_op jit(solution)/shard_map/ppermute | solution.py:515
  31.9 0.0 copy-done
  31.9 1.3 pack.2
  33.2 1.5 %collective-permute-start.1 = (bf16[128,2048]{1,0:T(8,128)(2,1)}, bf16[128,2048]{1,0:T(8,128)(2,1)S(1)}, u32[]{:S(2)}, u32[]{:S(2)}) collective-permute-start(bf16[128,2048]{1,0:T(8,128)(2,1)} %get-tuple-element.19), channel_id=1, source_target_pairs={{0,1},{1,2},{2,3},{3,0},{4,5},{5,6},{6,7},{7,4},{8,9},{9,10},{10,1... | collective-permute-start | bytes 1572872 | tf_op jit(solution)/shard_map/ppermute | solution.py:521
  34.7 1.8 %collective-permute-start.2 = (bf16[128,2048]{1,0:T(8,128)(2,1)}, bf16[128,2048]{1,0:T(8,128)(2,1)S(1)}, u32[]{:S(2)}, u32[]{:S(2)}) collective-permute-start(bf16[128,2048]{1,0:T(8,128)(2,1)} %get-tuple-element.22), channel_id=1, source_target_pairs={{0,3},{1,0},{2,1},{3,2},{4,7},{5,4},{6,5},{7,6},{8,11},{9,8},{10,9... | collective-permute-start | bytes 1572872 | tf_op jit(solution)/shard_map/ppermute | solution.py:521
  36.5 1.8 %collective-permute-start.6 = (bf16[128,2048]{1,0:T(8,128)(2,1)S(1)}, bf16[128,2048]{1,0:T(8,128)(2,1)S(1)}, u32[]{:S(2)}, u32[]{:S(2)}) collective-permute-start(bf16[128,2048]{1,0:T(8,128)(2,1)S(1)} %get-tuple-element.26), channel_id=1, source_target_pairs={{0,2},{1,3},{2,0},{3,1},{4,6},{5,7},{6,4},{7,5},{8,10},{9,11},{10,... | collective-permute-start | bytes 1572872 | tf_op jit(solution)/shard_map/ppermute | solution.py:521
  38.2 2.2 %pack.3 = (bf16[128,768]{1,0:T(8,128)(2,1)}, bf16[128,768]{1,0:T(8,128)(2,1)}, bf16[128,768]{1,0:T(8,128)(2,1)}, bf16[128,768]{1,0:T(8,128)(2,1)}, bf16[128,768]{1,0:T(8,128)(2,1)}) custom-call(s32[1]{0:T(128)} %bitcast.refs_0_.ctx_ref, bf16[1,128,12288]{2,1,0:T(8,128)(2,1)} %refs_1_.3), custom_call_target="tpu_custom_call" | custom-call | tf_op jit(solution)/shard_map/pack/pallas_call | solution.py:92
  40.4 0.6 collective-permute-start.3
  41.1 1.8 %collective-permute-start.4 = (bf16[128,768]{1,0:T(8,128)(2,1)}, bf16[128,768]{1,0:T(8,128)(2,1)S(1)}, u32[]{:S(2)}, u32[]{:S(2)}) collective-permute-start(bf16[128,768]{1,0:T(8,128)(2,1)} %get-tuple-element.24), channel_id=1, source_target_pairs={{0,5},{1,6},{2,7},{3,4},{4,1},{5,2},{6,3},{7,0},{8,13},{9,14},{10,... | collective-permute-start | bytes 589832 | tf_op jit(solution)/shard_map/ppermute | solution.py:521
  44.2 4.1 %collective-permute-done.3.refs_6_ = bf16[128,768]{1,0:T(8,128)(2,1)S(1)} collective-permute-done((bf16[128,768]{1,0:T(8,128)(2,1)}, bf16[128,768]{1,0:T(8,128)(2,1)S(1)}, u32[]{:S(2)}, u32[]{:S(2)}) %collective-permute-start.3) | collective-permute-done | bytes 196640 | tf_op jit(solution)/shard_map/ppermute | solution.py:521
  48.3 1.3 collective-permute-start.5
  49.6 3.1 %collective-permute-done.4.refs_7_ = bf16[128,768]{1,0:T(8,128)(2,1)S(1)} collective-permute-done((bf16[128,768]{1,0:T(8,128)(2,1)}, bf16[128,768]{1,0:T(8,128)(2,1)S(1)}, u32[]{:S(2)}, u32[]{:S(2)}) %collective-permute-start.4) | collective-permute-done | bytes 196640 | tf_op jit(solution)/shard_map/ppermute | solution.py:521
  52.7 2.2 %collective-permute-start.7 = (bf16[128,768]{1,0:T(8,128)(2,1)}, bf16[128,768]{1,0:T(8,128)(2,1)S(1)}, u32[]{:S(2)}, u32[]{:S(2)}) collective-permute-start(bf16[128,768]{1,0:T(8,128)(2,1)} %get-tuple-element.27), channel_id=1, source_target_pairs={{0,6},{1,7},{2,4},{3,5},{4,2},{5,3},{6,0},{7,1},{8,14},{9,15},{10,... | collective-permute-start | bytes 589832 | tf_op jit(solution)/shard_map/ppermute | solution.py:521
  54.8 3.1 %fusion = (f32[1024,128]{1,0:T(8,128)}, f32[1024,128]{1,0:T(8,128)}) fusion(f32[128]{0:T(128)S(1)} %get-tuple-element.38, f32[128]{0:T(128)S(1)} %get-tuple-element.39, f32[1024]{0:T(1024)S(1)} %add_convert_fusion), kind=kLoop, calls=%fused_computation.2 | loop fusion | flops 262144 | bytes 1053696 | tf_op jit(solution)/shard_map/mul | solution.py:531
  57.9 0.0 collective-permute-done.5.refs_8_
  57.9 3.1 %collective-permute-done.7.refs_10_ = bf16[128,768]{1,0:T(8,128)(2,1)S(1)} collective-permute-done((bf16[128,768]{1,0:T(8,128)(2,1)}, bf16[128,768]{1,0:T(8,128)(2,1)S(1)}, u32[]{:S(2)}, u32[]{:S(2)}) %collective-permute-start.7) | collective-permute-done | bytes 196640 | tf_op jit(solution)/shard_map/ppermute | solution.py:521
  61.1 0.0 collective-permute-done.1.refs_4_
  61.1 5.3 %collective-permute-done.2.refs_5_ = bf16[128,2048]{1,0:T(8,128)(2,1)S(1)} collective-permute-done((bf16[128,2048]{1,0:T(8,128)(2,1)}, bf16[128,2048]{1,0:T(8,128)(2,1)S(1)}, u32[]{:S(2)}, u32[]{:S(2)}) %collective-permute-start.2) | collective-permute-done | bytes 524320 | tf_op jit(solution)/shard_map/ppermute | solution.py:521
  66.4 1.7 %collective-permute-done.6.refs_9_ = bf16[128,2048]{1,0:T(8,128)(2,1)S(1)} collective-permute-done((bf16[128,2048]{1,0:T(8,128)(2,1)S(1)}, bf16[128,2048]{1,0:T(8,128)(2,1)S(1)}, u32[]{:S(2)}, u32[]{:S(2)}) %collective-permute-start.6) | collective-permute-done | bytes 524320 | tf_op jit(solution)/shard_map/ppermute | solution.py:521
  68.1 0.0 copy-done.12
  68.1 0.0 copy-done.14
  68.1 0.0 copy-done.8
  68.1 0.0 copy-done.9
  68.1 0.8 copy-done.10
  68.9 12.5 %attend.2 = (bf16[16,64,512]{2,1,0:T(8,128)(2,1)}, bf16[1024,512]{1,0:T(8,128)(2,1)}, bf16[1024,128]{1,0:T(8,128)(2,1)}, bf16[1024,128]{1,0:T(8,128)(2,1)}) custom-call(s32[1]{0:T(128)} %bitcast.refs_0_.ctx_ref, s32[16]{0:T(128)} %bitcast.15, s32[1]{0:T(128)S(6)} %copy.14.refs_2_, bf16[128,768]{1,0:T(8,128)(2,1)} %get-tuple-element.21.refs_3_, ...), custom_call_target="tpu_custom_call" | custom-call | flops 4400000000 | bytes 6000000 | tf_op jit(solution)/shard_map/attend/pallas_call | solution.py:280
  81.5 0.0 all-to-all-done.refs_3_
  81.5 3.8 %all-to-all-start.2 = ((bf16[8,128,512]{2,1,0:T(8,128)(2,1)}), bf16[8,128,512]{2,1,0:T(8,128)(2,1)S(1)}, u32[]{:S(2)}, u32[]{:S(2)}) async-start(bf16[8,128,512]{2,1,0:T(8,128)(2,1)} %bitcast.19), calls=%async_computation.2 | async-start | bytes 2097152 | tf_op jit(solution)/shard_map/all_to_all | solution.py:507
  85.3 11.6 %attend.3 = bf16[16,64,512]{2,1,0:T(8,128)(2,1)} custom-call(s32[1]{0:T(128)} %bitcast.refs_0_.ctx_ref, s32[16]{0:T(128)} %bitcast.16, s32[1]{0:T(128)S(6)} %copy.14.refs_2_, bf16[8,128,768]{2,1,0:T(8,128)(2,1)} %all-to-all-done.refs_3_, bf16[8,256,512]{2,1,0:T(8,128)(2,1)} %refs_4_.1, f32[1024,128]{1,0:T(8,128)} %get-tuple-element.37.refs_12_.refs_5_, ...), custom_call_target="tpu_custom_call" | custom-call | flops 4400000000 | bytes 6000000 | tf_op jit(solution)/shard_map/attend/pallas_call | solution.py:280
  96.9 0.0 copy-start.5
  96.9 0.0 copy-start.6
  97.0 0.0 copy-start.4
  97.0 1.1 all-to-all-done.2.part_ref
  98.1 4.4 %all-to-all-start.1 = ((bf16[8,128,512]{2,1,0:T(8,128)(2,1)}), bf16[8,128,512]{2,1,0:T(8,128)(2,1)S(1)}, u32[]{:S(2)}, u32[]{:S(2)}) async-start(bf16[8,128,512]{2,1,0:T(8,128)(2,1)} %bitcast.18), calls=%async_computation.1 | async-start | bytes 2097152 | tf_op jit(solution)/shard_map/all_to_all | solution.py:507
  102.5 0.0 copy-done.2
  102.6 1.0 pages.1.refs_0_
  103.6 0.1 collective-permute-start.10
  103.7 4.1 %collective-permute-start.8 = (bf16[2,288,128]{2,1,0:T(8,128)(2,1)S(1)}, bf16[2,288,128]{2,1,0:T(8,128)(2,1)S(1)}, u32[]{:S(2)}, u32[]{:S(2)}) collective-permute-start(bf16[2,288,128]{2,1,0:T(8,128)(2,1)S(1)} %pages.1.refs_0_), channel_id=1, source_target_pairs={{0,16},{8,24},{16,32},{24,40},{32,48},{40,56},{48,0},{56,8},{64,80... | collective-permute-start | bytes 442376 | tf_op jit(solution)/shard_map/ppermute | solution.py:498
  107.8 4.5 %collective-permute-start.9 = (bf16[2,288,128]{2,1,0:T(8,128)(2,1)S(1)}, bf16[2,288,128]{2,1,0:T(8,128)(2,1)S(1)}, u32[]{:S(2)}, u32[]{:S(2)}) collective-permute-start(bf16[2,288,128]{2,1,0:T(8,128)(2,1)S(1)} %pages.1.refs_0_), channel_id=1, source_target_pairs={{0,32},{8,40},{16,48},{24,56},{32,0},{40,8},{48,16},{56,24},{64,96... | collective-permute-start | bytes 442376 | tf_op jit(solution)/shard_map/ppermute | solution.py:498
  112.3 0.0 collective-permute-done.10.refs_3_
  112.3 11.9 %collective-permute-done.8.refs_1_ = bf16[2,288,128]{2,1,0:T(8,128)(2,1)S(1)} collective-permute-done((bf16[2,288,128]{2,1,0:T(8,128)(2,1)S(1)}, bf16[2,288,128]{2,1,0:T(8,128)(2,1)S(1)}, u32[]{:S(2)}, u32[]{:S(2)}) %collective-permute-start.8) | collective-permute-done | bytes 147488 | tf_op jit(solution)/shard_map/ppermute | solution.py:498
  124.2 6.5 %collective-permute-done.9.refs_2_ = bf16[2,288,128]{2,1,0:T(8,128)(2,1)S(1)} collective-permute-done((bf16[2,288,128]{2,1,0:T(8,128)(2,1)S(1)}, bf16[2,288,128]{2,1,0:T(8,128)(2,1)S(1)}, u32[]{:S(2)}, u32[]{:S(2)}) %collective-permute-start.9) | collective-permute-done | bytes 147488 | tf_op jit(solution)/shard_map/ppermute | solution.py:498
  130.7 0.0 copy-done.4
  130.7 2.1 %relay_pages.1 = (bf16[4,288,128]{2,1,0:T(8,128)(2,1)S(1)}, bf16[4,288,128]{2,1,0:T(8,128)(2,1)S(1)}, bf16[4,288,128]{2,1,0:T(8,128)(2,1)S(1)}, bf16[4,288,128]{2,1,0:T(8,128)(2,1)S(1)}) custom-call(s32[1]{0:T(128)} %bitcast.7.req_ref, s32[2,32]{1,0:T(2,128)S(1)} %bitcast.10, bf16[2,288,128]{2,1,0:T(8,128)(2,1)S(1)} %pages.1.refs_0_, ...), custom_call_target="tpu_custom_call" | custom-call | tf_op jit(solution)/shard_map/relay_pages/pallas_call | solution.py:418
  132.8 0.7 collective-permute-start.11
  133.5 2.3 %collective-permute-start.12 = (bf16[4,288,128]{2,1,0:T(8,128)(2,1)S(1)}, bf16[4,288,128]{2,1,0:T(8,128)(2,1)S(1)}, u32[]{:S(2)}, u32[]{:S(2)}) collective-permute-start(bf16[4,288,128]{2,1,0:T(8,128)(2,1)S(1)} %get-tuple-element.34), channel_id=1, source_target_pairs={{0,128},{8,136},{16,144},{24,152},{32,160},{40,168},{48,176},{56,1... | collective-permute-start | bytes 884744 | tf_op jit(solution)/shard_map/ppermute | solution.py:500
  135.8 0.0 collective-permute-start.13
  135.8 5.5 %collective-permute-done.11.refs_1_ = bf16[4,288,128]{2,1,0:T(8,128)(2,1)S(1)} collective-permute-done((bf16[4,288,128]{2,1,0:T(8,128)(2,1)S(1)}, bf16[4,288,128]{2,1,0:T(8,128)(2,1)S(1)}, u32[]{:S(2)}, u32[]{:S(2)}) %collective-permute-start.11) | collective-permute-done | bytes 294944 | tf_op jit(solution)/shard_map/ppermute | solution.py:500
  141.2 1.9 %collective-permute-done.12.refs_2_ = bf16[4,288,128]{2,1,0:T(8,128)(2,1)S(1)} collective-permute-done((bf16[4,288,128]{2,1,0:T(8,128)(2,1)S(1)}, bf16[4,288,128]{2,1,0:T(8,128)(2,1)S(1)}, u32[]{:S(2)}, u32[]{:S(2)}) %collective-permute-start.12) | collective-permute-done | bytes 294944 | tf_op jit(solution)/shard_map/ppermute | solution.py:500
  143.2 3.1 %collective-permute-done.13.refs_3_ = bf16[4,288,128]{2,1,0:T(8,128)(2,1)S(1)} collective-permute-done((bf16[4,288,128]{2,1,0:T(8,128)(2,1)S(1)}, bf16[4,288,128]{2,1,0:T(8,128)(2,1)S(1)}, u32[]{:S(2)}, u32[]{:S(2)}) %collective-permute-start.13) | collective-permute-done | bytes 294944 | tf_op jit(solution)/shard_map/ppermute | solution.py:500
  146.2 0.3 shard_map.95
  146.5 0.1 collective-permute-start.14
  146.6 1.4 collective-permute-done.14.crossed_ref
  148.0 0.3 shard_map.96
  148.3 0.7 reshape.71
  149.0 1.0 unpack.2.refs_0_
  150.0 0.0 all-to-all-done.1.part_ref
  150.0 1.0 unpack.3
  (20 shorter events, 0.1 us)
Async XLA Ops:
  0.6 8.5 %copy-start.7 = (bf16[1,128,576]{1,2,0:T(8,128)(2,1)S(1)}, bf16[1,128,576]{1,2,0:T(8,128)(2,1)}, u32[]{:S(2)}) copy-start(bf16[1,128,576]{1,2,0:T(8,128)(2,1)} %param.9) | copy-start | bytes 442372
  3.0 28.9 %copy-start = (bf16[1,128,12288]{2,1,0:T(8,128)(2,1)S(1)}, bf16[1,128,12288]{2,1,0:T(8,128)(2,1)}, u32[]{:S(2)}) copy-start(bf16[1,128,12288]{2,1,0:T(8,128)(2,1)} %refs_1_.3) | copy-start | bytes 9437188
  3.0 78.5 %all-to-all-start = ((bf16[8,128,768]{2,1,0:T(8,128)(2,1)}), bf16[8,128,768]{2,1,0:T(8,128)(2,1)}, u32[]{:S(2)}, u32[]{:S(2)}) async-start(bf16[8,128,768]{2,1,0:T(8,128)(2,1)} %pack_all.1), calls=%async_computation | async-start | bytes 3145728 | tf_op jit(solution)/shard_map/all_to_all | solution.py:507
  9.3 31.1 %copy-start.1 = (bf16[128,640]{1,0:T(8,128)(2,1)}, bf16[128,640]{1,0:T(8,128)(2,1)S(1)}, u32[]{:S(2)}) copy-start(bf16[128,640]{1,0:T(8,128)(2,1)S(1)} %pad.4.refs_2_.refs_15_.kv_ref) | copy-start | bytes 491524
  9.3 22.6 %collective-permute-start = (bf16[128,640]{1,0:T(8,128)(2,1)S(1)}, bf16[128,640]{1,0:T(8,128)(2,1)S(1)}, u32[]{:S(2)}, u32[]{:S(2)}) collective-permute-start(bf16[128,640]{1,0:T(8,128)(2,1)S(1)} %pad.4.refs_2_.refs_15_.kv_ref), channel_id=1, source_target_pairs={{0,4},{1,5},{2,6},{3,7},{4,0},{5,1},{6,2},{7,3},{8,12},{9,13},{10,... | collective-permute-start | bytes 491528 | tf_op jit(solution)/shard_map/ppermute | solution.py:515
  31.9 8.5 %copy-start.3 = (bf16[128,640]{1,0:T(8,128)(2,1)}, bf16[128,640]{1,0:T(8,128)(2,1)S(1)}, u32[]{:S(2)}) copy-start(bf16[128,640]{1,0:T(8,128)(2,1)S(1)} %collective-permute-done.refs_3_.refs_16_) | copy-start | bytes 491524
  33.2 27.9 %collective-permute-start.1 = (bf16[128,2048]{1,0:T(8,128)(2,1)}, bf16[128,2048]{1,0:T(8,128)(2,1)S(1)}, u32[]{:S(2)}, u32[]{:S(2)}) collective-permute-start(bf16[128,2048]{1,0:T(8,128)(2,1)} %get-tuple-element.19), channel_id=1, source_target_pairs={{0,1},{1,2},{2,3},{3,0},{4,5},{5,6},{6,7},{7,4},{8,9},{9,10},{10,1... | collective-permute-start | bytes 1572872 | tf_op jit(solution)/shard_map/ppermute | solution.py:521
  34.7 31.7 %collective-permute-start.2 = (bf16[128,2048]{1,0:T(8,128)(2,1)}, bf16[128,2048]{1,0:T(8,128)(2,1)S(1)}, u32[]{:S(2)}, u32[]{:S(2)}) collective-permute-start(bf16[128,2048]{1,0:T(8,128)(2,1)} %get-tuple-element.22), channel_id=1, source_target_pairs={{0,3},{1,0},{2,1},{3,2},{4,7},{5,4},{6,5},{7,6},{8,11},{9,8},{10,9... | collective-permute-start | bytes 1572872 | tf_op jit(solution)/shard_map/ppermute | solution.py:521
  36.5 31.6 %collective-permute-start.6 = (bf16[128,2048]{1,0:T(8,128)(2,1)S(1)}, bf16[128,2048]{1,0:T(8,128)(2,1)S(1)}, u32[]{:S(2)}, u32[]{:S(2)}) collective-permute-start(bf16[128,2048]{1,0:T(8,128)(2,1)S(1)} %get-tuple-element.26), channel_id=1, source_target_pairs={{0,2},{1,3},{2,0},{3,1},{4,6},{5,7},{6,4},{7,5},{8,10},{9,11},{10,... | collective-permute-start | bytes 1572872 | tf_op jit(solution)/shard_map/ppermute | solution.py:521
  40.4 7.9 %collective-permute-start.3 = (bf16[128,768]{1,0:T(8,128)(2,1)}, bf16[128,768]{1,0:T(8,128)(2,1)S(1)}, u32[]{:S(2)}, u32[]{:S(2)}) collective-permute-start(bf16[128,768]{1,0:T(8,128)(2,1)} %get-tuple-element.23), channel_id=1, source_target_pairs={{0,4},{1,5},{2,6},{3,7},{4,0},{5,1},{6,2},{7,3},{8,12},{9,13},{10,... | collective-permute-start | bytes 589832 | tf_op jit(solution)/shard_map/ppermute | solution.py:521
  41.1 11.6 %collective-permute-start.4 = (bf16[128,768]{1,0:T(8,128)(2,1)}, bf16[128,768]{1,0:T(8,128)(2,1)S(1)}, u32[]{:S(2)}, u32[]{:S(2)}) collective-permute-start(bf16[128,768]{1,0:T(8,128)(2,1)} %get-tuple-element.24), channel_id=1, source_target_pairs={{0,5},{1,6},{2,7},{3,4},{4,1},{5,2},{6,3},{7,0},{8,13},{9,14},{10,... | collective-permute-start | bytes 589832 | tf_op jit(solution)/shard_map/ppermute | solution.py:521
  48.3 19.8 %copy-start.11 = (bf16[128,768]{1,0:T(8,128)(2,1)}, bf16[128,768]{1,0:T(8,128)(2,1)S(1)}, u32[]{:S(2)}) copy-start(bf16[128,768]{1,0:T(8,128)(2,1)S(1)} %collective-permute-done.3.refs_6_) | copy-start | bytes 589828
  48.3 9.6 %collective-permute-start.5 = (bf16[128,768]{1,0:T(8,128)(2,1)}, bf16[128,768]{1,0:T(8,128)(2,1)S(1)}, u32[]{:S(2)}, u32[]{:S(2)}) collective-permute-start(bf16[128,768]{1,0:T(8,128)(2,1)} %get-tuple-element.25), channel_id=1, source_target_pairs={{0,7},{1,4},{2,5},{3,6},{4,3},{5,0},{6,1},{7,2},{8,15},{9,12},{10,... | collective-permute-start | bytes 589832 | tf_op jit(solution)/shard_map/ppermute | solution.py:521
  52.7 15.4 %copy-start.12 = (bf16[128,768]{1,0:T(8,128)(2,1)}, bf16[128,768]{1,0:T(8,128)(2,1)S(1)}, u32[]{:S(2)}) copy-start(bf16[128,768]{1,0:T(8,128)(2,1)S(1)} %collective-permute-done.4.refs_7_) | copy-start | bytes 589828
  52.7 8.4 %collective-permute-start.7 = (bf16[128,768]{1,0:T(8,128)(2,1)}, bf16[128,768]{1,0:T(8,128)(2,1)S(1)}, u32[]{:S(2)}, u32[]{:S(2)}) collective-permute-start(bf16[128,768]{1,0:T(8,128)(2,1)} %get-tuple-element.27), channel_id=1, source_target_pairs={{0,6},{1,7},{2,4},{3,5},{4,2},{5,3},{6,0},{7,1},{8,14},{9,15},{10,... | collective-permute-start | bytes 589832 | tf_op jit(solution)/shard_map/ppermute | solution.py:521
  57.9 10.2 %copy-start.13 = (bf16[128,768]{1,0:T(8,128)(2,1)}, bf16[128,768]{1,0:T(8,128)(2,1)S(1)}, u32[]{:S(2)}) copy-start(bf16[128,768]{1,0:T(8,128)(2,1)S(1)} %collective-permute-done.5.refs_8_) | copy-start | bytes 589828
  61.1 7.1 %copy-start.14 = (bf16[128,768]{1,0:T(8,128)(2,1)}, bf16[128,768]{1,0:T(8,128)(2,1)S(1)}, u32[]{:S(2)}) copy-start(bf16[128,768]{1,0:T(8,128)(2,1)S(1)} %collective-permute-done.7.refs_10_) | copy-start | bytes 589828
  61.1 7.1 %copy-start.8 = (bf16[128,2048]{1,0:T(8,128)(2,1)}, bf16[128,2048]{1,0:T(8,128)(2,1)S(1)}, u32[]{:S(2)}) copy-start(bf16[128,2048]{1,0:T(8,128)(2,1)S(1)} %collective-permute-done.1.refs_4_) | copy-start | bytes 1572868
  66.4 1.7 %copy-start.9 = (bf16[128,2048]{1,0:T(8,128)(2,1)}, bf16[128,2048]{1,0:T(8,128)(2,1)S(1)}, u32[]{:S(2)}) copy-start(bf16[128,2048]{1,0:T(8,128)(2,1)S(1)} %collective-permute-done.2.refs_5_) | copy-start | bytes 1572868
  68.1 0.8 copy-start.10
  81.5 16.6 %all-to-all-start.2 = ((bf16[8,128,512]{2,1,0:T(8,128)(2,1)}), bf16[8,128,512]{2,1,0:T(8,128)(2,1)S(1)}, u32[]{:S(2)}, u32[]{:S(2)}) async-start(bf16[8,128,512]{2,1,0:T(8,128)(2,1)} %bitcast.19), calls=%async_computation.2 | async-start | bytes 2097152 | tf_op jit(solution)/shard_map/all_to_all | solution.py:507
  96.9 5.6 %copy-start.2 = (bf16[128,640]{1,0:T(8,128)(2,1)S(1)}, bf16[128,640]{1,0:T(8,128)(2,1)}, u32[]{:S(2)}) copy-start(bf16[128,640]{1,0:T(8,128)(2,1)} %copy-done.1) | copy-start | bytes 491524
  96.9 5.6 %copy-start.5 = (f32[512]{0:T(512)S(1)}, f32[512]{0:T(512)}, u32[]{:S(2)}) copy-start(f32[512]{0:T(512)} %param.10) | copy-start | bytes 6148
  96.9 5.6 %copy-start.6 = (s32[1,16]{1,0:T(1,128)S(1)}, s32[1,16]{1,0:T(1,128)}, u32[]{:S(2)}) copy-start(s32[1,16]{1,0:T(1,128)} %param.14) | copy-start | bytes 196
  97.0 33.7 %copy-start.4 = (s32[32,2]{0,1:T(2,128)S(1)}, s32[32,2]{0,1:T(2,128)}, u32[]{:S(2)}) copy-start(s32[32,2]{0,1:T(2,128)} %param.15) | copy-start | bytes 772
  98.1 51.9 %all-to-all-start.1 = ((bf16[8,128,512]{2,1,0:T(8,128)(2,1)}), bf16[8,128,512]{2,1,0:T(8,128)(2,1)S(1)}, u32[]{:S(2)}, u32[]{:S(2)}) async-start(bf16[8,128,512]{2,1,0:T(8,128)(2,1)} %bitcast.18), calls=%async_computation.1 | async-start | bytes 2097152 | tf_op jit(solution)/shard_map/all_to_all | solution.py:507
  103.6 8.7 %collective-permute-start.10 = (bf16[2,288,128]{2,1,0:T(8,128)(2,1)S(1)}, bf16[2,288,128]{2,1,0:T(8,128)(2,1)S(1)}, u32[]{:S(2)}, u32[]{:S(2)}) collective-permute-start(bf16[2,288,128]{2,1,0:T(8,128)(2,1)S(1)} %pages.1.refs_0_), channel_id=1, source_target_pairs={{0,48},{8,56},{16,0},{24,8},{32,16},{40,24},{48,32},{56,40},{64,11... | collective-permute-start | bytes 442376 | tf_op jit(solution)/shard_map/ppermute | solution.py:498
  103.7 20.5 %collective-permute-start.8 = (bf16[2,288,128]{2,1,0:T(8,128)(2,1)S(1)}, bf16[2,288,128]{2,1,0:T(8,128)(2,1)S(1)}, u32[]{:S(2)}, u32[]{:S(2)}) collective-permute-start(bf16[2,288,128]{2,1,0:T(8,128)(2,1)S(1)} %pages.1.refs_0_), channel_id=1, source_target_pairs={{0,16},{8,24},{16,32},{24,40},{32,48},{40,56},{48,0},{56,8},{64,80... | collective-permute-start | bytes 442376 | tf_op jit(solution)/shard_map/ppermute | solution.py:498
  107.8 22.9 %collective-permute-start.9 = (bf16[2,288,128]{2,1,0:T(8,128)(2,1)S(1)}, bf16[2,288,128]{2,1,0:T(8,128)(2,1)S(1)}, u32[]{:S(2)}, u32[]{:S(2)}) collective-permute-start(bf16[2,288,128]{2,1,0:T(8,128)(2,1)S(1)} %pages.1.refs_0_), channel_id=1, source_target_pairs={{0,32},{8,40},{16,48},{24,56},{32,0},{40,8},{48,16},{56,24},{64,96... | collective-permute-start | bytes 442376 | tf_op jit(solution)/shard_map/ppermute | solution.py:498
  132.8 8.4 %collective-permute-start.11 = (bf16[4,288,128]{2,1,0:T(8,128)(2,1)S(1)}, bf16[4,288,128]{2,1,0:T(8,128)(2,1)S(1)}, u32[]{:S(2)}, u32[]{:S(2)}) collective-permute-start(bf16[4,288,128]{2,1,0:T(8,128)(2,1)S(1)} %get-tuple-element.33), channel_id=1, source_target_pairs={{0,64},{8,72},{16,80},{24,88},{32,96},{40,104},{48,112},{56,120},{... | collective-permute-start | bytes 884744 | tf_op jit(solution)/shard_map/ppermute | solution.py:500
  133.5 9.7 %collective-permute-start.12 = (bf16[4,288,128]{2,1,0:T(8,128)(2,1)S(1)}, bf16[4,288,128]{2,1,0:T(8,128)(2,1)S(1)}, u32[]{:S(2)}, u32[]{:S(2)}) collective-permute-start(bf16[4,288,128]{2,1,0:T(8,128)(2,1)S(1)} %get-tuple-element.34), channel_id=1, source_target_pairs={{0,128},{8,136},{16,144},{24,152},{32,160},{40,168},{48,176},{56,1... | collective-permute-start | bytes 884744 | tf_op jit(solution)/shard_map/ppermute | solution.py:500
  135.8 10.4 %collective-permute-start.13 = (bf16[4,288,128]{2,1,0:T(8,128)(2,1)S(1)}, bf16[4,288,128]{2,1,0:T(8,128)(2,1)S(1)}, u32[]{:S(2)}, u32[]{:S(2)}) collective-permute-start(bf16[4,288,128]{2,1,0:T(8,128)(2,1)S(1)} %get-tuple-element.35), channel_id=1, source_target_pairs={{0,192},{8,200},{16,208},{24,216},{32,224},{40,232},{48,240},{56,2... | collective-permute-start | bytes 884744 | tf_op jit(solution)/shard_map/ppermute | solution.py:500
  146.5 1.5 collective-permute-start.14

commit v3 on v2

--- a/solution.py
+++ b/solution.py
@@ -52,6 +52,10 @@
 
 def forward(k):
     return [(d, partner(d, k)) for d in range(GROUPS)]
+
+
+def backward(k):
+    return [(partner(d, k), d) for d in range(GROUPS)]
 
 
 def params(limit):
@@ -138,7 +142,8 @@
         arrived, refs = refs[:GROUPS], refs[GROUPS:]
         w_hbm, cos_hbm, sin_hbm, gain_ref, kv_hbm, kvz_hbm, o_ref, cs_hbm, krl_hbm, krr_hbm, *refs = refs
     else:
-        stacked, w_hbm, cos_hbm, sin_hbm, cs_hbm, krl_hbm, krr_hbm, o_ref, *refs = refs
+        stacked, w_hbm, cos_hbm, sin_hbm, cs_hbm, krl_hbm, krr_hbm, *refs = refs
+        outs, refs = refs[:GROUPS], refs[GROUPS:]
         arrived = [stacked.at[k] for k in range(GROUPS)]
     w_ref, cs, krl, krr, cos_ref, sin_ref, qs, os, k0, k1, v, sems, out_sems = refs
     total = cs.shape[0]
@@ -164,6 +169,14 @@
             place = pl.multiple_of(order_ref[2 * source + i] * BLK, BLK)
             places.append((2 * source + i, place))
             moves.append((k, pl.ds(i * BLK, BLK), pl.ds(place, BLK)))
+    targets = []
+    for n, (block, place) in enumerate(places):
+        if first:
+            targets.append((place, o_ref.at[block]))
+        else:
+            k, i = n // 2, n % 2
+            place = pl.multiple_of(order_ref[2 * partner(context, k, back=True) + i] * BLK, BLK)
+            targets.append((place, outs[k].at[pl.ds(i * BLK, BLK)]))
     keys_here = []
     if first:
         for k, here, there in moves:
@@ -259,12 +272,10 @@
             if n + 1 < len(items):
                 ahead = score(pair, *items[n + 1])
             weigh(pair, *item, scores)
-        for n, (block, place) in enumerate(places):
-            columns = pl.ds(pair * (2 * HD), 2 * HD)
+        columns = pl.ds(pair * (2 * HD), 2 * HD)
+        for n, (place, target) in enumerate(targets):
             stores.append(
-                pltpu.make_async_copy(
-                    os.at[pair, pl.ds(place, BLK)], o_ref.at[block, :, columns], out_sems.at[pair, n]
-                )
+                pltpu.make_async_copy(os.at[pair, pl.ds(place, BLK)], target.at[:, columns], out_sems.at[pair, n])
             )
             stores[-1].start()
     for copy in stores + kept:
@@ -274,7 +285,10 @@
 def attend(chunk, context, order_row, length, arrived, kv_up, extra):
     first = chunk == 0
     total = GROUPS * LOCAL
-    shapes = [(2 * GROUPS, BLK, OPART)] + [(total, LAT), (total, 128), (total, 128)] * first
+    if first:
+        shapes = [(2 * GROUPS, BLK, OPART), (total, LAT), (total, 128), (total, 128)]
+    else:
+        shapes = [(LOCAL, OPART)] * GROUPS
     n_arrived = len(arrived)
     sides = [ANY, ANY, VMEM, ANY, ANY] if first else [ANY] * 5
     outs = pl.pallas_call(
@@ -303,32 +317,38 @@
         ),
         name="attend",
     )(context, order_row, length, *arrived, kv_up, *extra)
-    return outs[0].reshape(GROUPS, LOCAL, OPART), outs[1:]
-
-
-def unpack_kernel(chunk, part_ref, *refs):
+    if first:
+        return outs[0].reshape(GROUPS, LOCAL, OPART), outs[1:]
+    return outs, ()
+
+
+def unpack_kernel(chunk, ctx_ref, *refs):
     o_ref, sems = refs[-2:]
     stores = []
-    for j in range(GROUPS):
-        columns = pl.ds(j * (8 * HD) + chunk * OPART, OPART)
-        stores.append(pltpu.make_async_copy(part_ref.at[j], o_ref.at[0, :, columns], sems.at[j]))
+    for n in range(GROUPS):
+        if chunk == 0:
+            part, group = refs[0].at[n], n
+        else:
+            part, group = refs[n], partner(ctx_ref[0], n)
+        columns = pl.ds(pl.multiple_of(group * (8 * HD) + chunk * OPART, 128), OPART)
+        stores.append(pltpu.make_async_copy(part, o_ref.at[0, :, columns], sems.at[n]))
         stores[-1].start()
     for store in stores:
         store.wait()
 
 
-def unpack(chunk, part, out):
+def unpack(chunk, context, parts, out):
     more = [] if out is None else [out]
     return pl.pallas_call(
         functools.partial(unpack_kernel, chunk),
-        in_specs=[VMEM] + [ANY] * len(more),
+        in_specs=[SMEM] + [VMEM] * len(parts) + [ANY] * len(more),
         out_specs=ANY,
         out_shape=jax.ShapeDtypeStruct((1, LOCAL, HEADS * HD), jnp.bfloat16),
         scratch_shapes=[pltpu.SemaphoreType.DMA((GROUPS,))],
-        input_output_aliases={1: 0} if more else {},
+        input_output_aliases={1 + len(parts): 0} if more else {},
         compiler_params=params(8),
         name="unpack",
-    )(part, *more)
+    )(context, *parts, *more)
 
 
 def pages_kernel(ctx_ref, order_ref, offset_ref, kv_ref, gain_ref, freq_ref, o_ref, rows, page):
@@ -533,7 +553,11 @@
     for chunk in range(CHUNKS):
         out, kept = attend(chunk, context, order_row, lengths, arrived[chunk], kv_up, extra)
         extra = extra[:2] + list(kept) if chunk == 0 else extra
-        attn_out = unpack(chunk, exchange(out), attn_out)
+        if chunk == 0:
+            parts = [exchange(out)]
+        else:
+            parts = [out[0]] + [lax.ppermute(out[k], "ctx", backward(k)) for k in range(1, GROUPS)]
+        attn_out = unpack(chunk, context, parts, attn_out)
     return attn_out, shipped
 
 

time: 154 us -> 164 us (1.065)
  starting transfers between devices: 39.1 us -> 45.4 us
  waiting for transfers between devices: 69.2 us -> 71.9 us
    ppermute x0 -> x7, starting transfers between devices: none -> 12 us  [body(): lax.ppermute(out[k], 'ctx', backward(k))]
    ppermute x0 -> x7, waiting for transfers between devices: none -> 5.8 us  [body(): lax.ppermute(out[k], 'ctx', backward(k))]
    all_to_all x3 -> x2, starting transfers between devices: 14.3 us -> 9.8 us  [exchange(): return lax.all_to_all(array, 'ctx', split_axis=0, concat_axis=0, tiled=True)]
  transfers between devices with their start and end apart: 18 -> 24, of which waited for: 13 -> 16; matrix products, arithmetic and copies ran while one was open for 3% -> 2% of each run, Pallas kernels for 21% -> 20%
where the time goes in v3:
time: 164 us; the launch traced here: 160 us
  waiting for transfers between devices  71.9 us (44%)
  starting transfers between devices  45.4 us (28%)
  Pallas kernels  35.9 us (22%)
  other arithmetic  3.1 us (2%)
  between operations  2.41 us (1%)
  local copies, waits for them, and re-layouts  1.72 us (1%)
    pallas_call x2, Pallas kernels, attend(): pl.pallas_call(functools.partial(attend_kernel, chunk), in_specs=[SMEM, S...  24.2 us
    ppermute x1, waiting for transfers between devices, body(): beyond = lax.ppermute(padded, 'ctx', forward(3))  20.5 us
    ppermute x3, waiting for transfers between devices, ship(): lax.ppermute(pages, 'req', along_z(d))  18.8 us
    ppermute x7, waiting for transfers between devices, body(): lax.ppermute(sent[k], 'ctx', forward(k))  17.4 us
    ppermute x7, starting transfers between devices, body(): lax.ppermute(out[k], 'ctx', backward(k))  12 us
    ppermute x7, starting transfers between devices, body(): lax.ppermute(sent[k], 'ctx', forward(k))  11 us
    all_to_all x2, starting transfers between devices, exchange(): return lax.all_to_all(array, 'ctx', split_axis=0, concat_axis=0, tiled=True)  9.8 us
    ppermute x3, waiting for transfers between devices, ship(): lax.ppermute(outgoing[d], 'req', along_x(d))  9.47 us
  transfers between devices with their start and end apart: 24, of which 16 were waited for; matrix products, arithmetic and copies ran while one was open for 2% of the time, Pallas kernels for 20%

profile of v3, /device:TPU:70, one launch (start us, length us, event | category | flops | bytes accessed | tf_op | source)
XLA Modules:
  0.0 160.5 jit_solution(12147241659284897991)
XLA Ops:
  0.6 2.3 %pack_all.1 = bf16[8,128,768]{2,1,0:T(8,128)(2,1)} custom-call(bf16[1,128,12288]{2,1,0:T(8,128)(2,1)} %refs_1_.3), custom_call_target="tpu_custom_call" | custom-call | tf_op jit(solution)/shard_map/pack_all/pallas_call | solution.py:127
  3.0 0.0 copy-start
  3.0 6.1 %all-to-all-start = ((bf16[8,128,768]{2,1,0:T(8,128)(2,1)}), bf16[8,128,768]{2,1,0:T(8,128)(2,1)}, u32[]{:S(2)}, u32[]{:S(2)}) async-start(bf16[8,128,768]{2,1,0:T(8,128)(2,1)} %pack_all.1), calls=%async_computation | async-start | bytes 3145728 | tf_op jit(solution)/shard_map/all_to_all | solution.py:527
  9.1 0.2 copy.11
  9.3 2.1 %collective-permute-start = (bf16[128,640]{1,0:T(8,128)(2,1)S(1)}, bf16[128,640]{1,0:T(8,128)(2,1)S(1)}, u32[]{:S(2)}, u32[]{:S(2)}) collective-permute-start(bf16[128,640]{1,0:T(8,128)(2,1)S(1)} %pad.4.refs_2_.refs_15_.kv_ref), channel_id=1, source_target_pairs={{0,4},{1,5},{2,6},{3,7},{4,0},{5,1},{6,2},{7,3},{8,12},{9,13},{10,... | collective-permute-start | bytes 491528 | tf_op jit(solution)/shard_map/ppermute | solution.py:535
  11.4 20.5 %collective-permute-done.refs_3_.refs_16_ = bf16[128,640]{1,0:T(8,128)(2,1)S(1)} collective-permute-done((bf16[128,640]{1,0:T(8,128)(2,1)S(1)}, bf16[128,640]{1,0:T(8,128)(2,1)S(1)}, u32[]{:S(2)}, u32[]{:S(2)}) %collective-permute-start) | collective-permute-done | bytes 163872 | tf_op jit(solution)/shard_map/ppermute | solution.py:535
  31.9 1.3 pack.2
  33.2 1.5 collective-permute-start.1
  34.7 1.8 %collective-permute-start.2 = (bf16[128,2048]{1,0:T(8,128)(2,1)}, bf16[128,2048]{1,0:T(8,128)(2,1)S(1)}, u32[]{:S(2)}, u32[]{:S(2)}) collective-permute-start(bf16[128,2048]{1,0:T(8,128)(2,1)} %get-tuple-element.30), channel_id=1, source_target_pairs={{0,3},{1,0},{2,1},{3,2},{4,7},{5,4},{6,5},{7,6},{8,11},{9,8},{10,9... | collective-permute-start | bytes 1572872 | tf_op jit(solution)/shard_map/ppermute | solution.py:541
  36.5 1.8 %collective-permute-start.6 = (bf16[128,2048]{1,0:T(8,128)(2,1)S(1)}, bf16[128,2048]{1,0:T(8,128)(2,1)S(1)}, u32[]{:S(2)}, u32[]{:S(2)}) collective-permute-start(bf16[128,2048]{1,0:T(8,128)(2,1)S(1)} %get-tuple-element.34), channel_id=1, source_target_pairs={{0,2},{1,3},{2,0},{3,1},{4,6},{5,7},{6,4},{7,5},{8,10},{9,11},{10,... | collective-permute-start | bytes 1572872 | tf_op jit(solution)/shard_map/ppermute | solution.py:541
  38.3 2.2 %pack.3 = (bf16[128,768]{1,0:T(8,128)(2,1)}, bf16[128,768]{1,0:T(8,128)(2,1)}, bf16[128,768]{1,0:T(8,128)(2,1)}, bf16[128,768]{1,0:T(8,128)(2,1)}, bf16[128,768]{1,0:T(8,128)(2,1)}) custom-call(s32[1]{0:T(128)} %bitcast.refs_0_.ctx_ref, bf16[1,128,12288]{2,1,0:T(8,128)(2,1)} %refs_1_.3), custom_call_target="tpu_custom_call" | custom-call | tf_op jit(solution)/shard_map/pack/pallas_call | solution.py:96
  40.5 0.6 collective-permute-start.3
  41.1 1.8 %collective-permute-start.4 = (bf16[128,768]{1,0:T(8,128)(2,1)}, bf16[128,768]{1,0:T(8,128)(2,1)S(1)}, u32[]{:S(2)}, u32[]{:S(2)}) collective-permute-start(bf16[128,768]{1,0:T(8,128)(2,1)} %get-tuple-element.32), channel_id=1, source_target_pairs={{0,5},{1,6},{2,7},{3,4},{4,1},{5,2},{6,3},{7,0},{8,13},{9,14},{10,... | collective-permute-start | bytes 589832 | tf_op jit(solution)/shard_map/ppermute | solution.py:541
  44.2 4.1 %collective-permute-done.3.refs_6_ = bf16[128,768]{1,0:T(8,128)(2,1)S(1)} collective-permute-done((bf16[128,768]{1,0:T(8,128)(2,1)}, bf16[128,768]{1,0:T(8,128)(2,1)S(1)}, u32[]{:S(2)}, u32[]{:S(2)}) %collective-permute-start.3) | collective-permute-done | bytes 196640 | tf_op jit(solution)/shard_map/ppermute | solution.py:541
  48.3 1.3 collective-permute-start.5
  49.7 3.1 %collective-permute-done.4.refs_7_ = bf16[128,768]{1,0:T(8,128)(2,1)S(1)} collective-permute-done((bf16[128,768]{1,0:T(8,128)(2,1)}, bf16[128,768]{1,0:T(8,128)(2,1)S(1)}, u32[]{:S(2)}, u32[]{:S(2)}) %collective-permute-start.4) | collective-permute-done | bytes 196640 | tf_op jit(solution)/shard_map/ppermute | solution.py:541
  52.7 2.2 %collective-permute-start.7 = (bf16[128,768]{1,0:T(8,128)(2,1)}, bf16[128,768]{1,0:T(8,128)(2,1)S(1)}, u32[]{:S(2)}, u32[]{:S(2)}) collective-permute-start(bf16[128,768]{1,0:T(8,128)(2,1)} %get-tuple-element.35), channel_id=1, source_target_pairs={{0,6},{1,7},{2,4},{3,5},{4,2},{5,3},{6,0},{7,1},{8,14},{9,15},{10,... | collective-permute-start | bytes 589832 | tf_op jit(solution)/shard_map/ppermute | solution.py:541
  54.9 3.1 %fusion = (f32[1024,128]{1,0:T(8,128)}, f32[1024,128]{1,0:T(8,128)}) fusion(f32[128]{0:T(128)S(1)} %get-tuple-element.54, f32[128]{0:T(128)S(1)} %get-tuple-element.55, f32[1024]{0:T(1024)S(1)} %add_convert_fusion), kind=kLoop, calls=%fused_computation.2 | loop fusion | flops 262144 | bytes 1053696 | tf_op jit(solution)/shard_map/mul | solution.py:551
  58.0 0.0 collective-permute-done.5.refs_8_
  58.0 3.1 %collective-permute-done.7.refs_10_ = bf16[128,768]{1,0:T(8,128)(2,1)S(1)} collective-permute-done((bf16[128,768]{1,0:T(8,128)(2,1)}, bf16[128,768]{1,0:T(8,128)(2,1)S(1)}, u32[]{:S(2)}, u32[]{:S(2)}) %collective-permute-start.7) | collective-permute-done | bytes 196640 | tf_op jit(solution)/shard_map/ppermute | solution.py:541
  61.1 0.0 collective-permute-done.1.refs_4_
  61.1 5.3 %collective-permute-done.2.refs_5_ = bf16[128,2048]{1,0:T(8,128)(2,1)S(1)} collective-permute-done((bf16[128,2048]{1,0:T(8,128)(2,1)}, bf16[128,2048]{1,0:T(8,128)(2,1)S(1)}, u32[]{:S(2)}, u32[]{:S(2)}) %collective-permute-start.2) | collective-permute-done | bytes 524320 | tf_op jit(solution)/shard_map/ppermute | solution.py:541
  66.5 1.7 %collective-permute-done.6.refs_9_ = bf16[128,2048]{1,0:T(8,128)(2,1)S(1)} collective-permute-done((bf16[128,2048]{1,0:T(8,128)(2,1)S(1)}, bf16[128,2048]{1,0:T(8,128)(2,1)S(1)}, u32[]{:S(2)}, u32[]{:S(2)}) %collective-permute-start.6) | collective-permute-done | bytes 524320 | tf_op jit(solution)/shard_map/ppermute | solution.py:541
  68.2 0.8 copy-done.11
  69.0 12.6 %attend.2 = (bf16[16,64,512]{2,1,0:T(8,128)(2,1)}, bf16[1024,512]{1,0:T(8,128)(2,1)}, bf16[1024,128]{1,0:T(8,128)(2,1)}, bf16[1024,128]{1,0:T(8,128)(2,1)}) custom-call(s32[1]{0:T(128)} %bitcast.refs_0_.ctx_ref, s32[16]{0:T(128)} %bitcast.14, s32[1]{0:T(128)S(6)} %copy.14.refs_2_, bf16[128,768]{1,0:T(8,128)(2,1)} %get-tuple-element.29.refs_3_, ...), custom_call_target="tpu_custom_call" | custom-call | flops 4400000000 | bytes 6000000 | tf_op jit(solution)/shard_map/attend/pallas_call | solution.py:294
  81.5 0.0 copy-start.6
  81.5 0.0 copy-start.7
  81.6 0.0 copy-start.5
  81.6 3.7 %all-to-all-start.1 = ((bf16[8,128,512]{2,1,0:T(8,128)(2,1)}), bf16[8,128,512]{2,1,0:T(8,128)(2,1)S(1)}, u32[]{:S(2)}, u32[]{:S(2)}) async-start(bf16[8,128,512]{2,1,0:T(8,128)(2,1)} %bitcast.17), calls=%async_computation.1 | async-start | bytes 2097152 | tf_op jit(solution)/shard_map/all_to_all | solution.py:527
  85.3 1.0 pages.1.refs_0_
  86.3 3.7 %collective-permute-start.15 = (bf16[2,288,128]{2,1,0:T(8,128)(2,1)S(1)}, bf16[2,288,128]{2,1,0:T(8,128)(2,1)S(1)}, u32[]{:S(2)}, u32[]{:S(2)}) collective-permute-start(bf16[2,288,128]{2,1,0:T(8,128)(2,1)S(1)} %pages.1.refs_0_), channel_id=1, source_target_pairs={{0,16},{8,24},{16,32},{24,40},{32,48},{40,56},{48,0},{56,8},{64,80... | collective-permute-start | bytes 442376 | tf_op jit(solution)/shard_map/ppermute | solution.py:518
  90.0 1.0 collective-permute-start.16
  91.0 2.8 %collective-permute-start.17 = (bf16[2,288,128]{2,1,0:T(8,128)(2,1)S(1)}, bf16[2,288,128]{2,1,0:T(8,128)(2,1)S(1)}, u32[]{:S(2)}, u32[]{:S(2)}) collective-permute-start(bf16[2,288,128]{2,1,0:T(8,128)(2,1)S(1)} %pages.1.refs_0_), channel_id=1, source_target_pairs={{0,48},{8,56},{16,0},{24,8},{32,16},{40,24},{48,32},{56,40},{64,11... | collective-permute-start | bytes 442376 | tf_op jit(solution)/shard_map/ppermute | solution.py:518
  93.8 12.3 %collective-permute-done.15.refs_1_ = bf16[2,288,128]{2,1,0:T(8,128)(2,1)S(1)} collective-permute-done((bf16[2,288,128]{2,1,0:T(8,128)(2,1)S(1)}, bf16[2,288,128]{2,1,0:T(8,128)(2,1)S(1)}, u32[]{:S(2)}, u32[]{:S(2)}) %collective-permute-start.15) | collective-permute-done | bytes 147488 | tf_op jit(solution)/shard_map/ppermute | solution.py:518
  106.1 6.5 %collective-permute-done.16.refs_2_ = bf16[2,288,128]{2,1,0:T(8,128)(2,1)S(1)} collective-permute-done((bf16[2,288,128]{2,1,0:T(8,128)(2,1)S(1)}, bf16[2,288,128]{2,1,0:T(8,128)(2,1)S(1)}, u32[]{:S(2)}, u32[]{:S(2)}) %collective-permute-start.16) | collective-permute-done | bytes 147488 | tf_op jit(solution)/shard_map/ppermute | solution.py:518
  112.6 0.0 collective-permute-done.17.refs_3_
  112.6 2.3 %relay_pages.1 = (bf16[4,288,128]{2,1,0:T(8,128)(2,1)S(1)}, bf16[4,288,128]{2,1,0:T(8,128)(2,1)S(1)}, bf16[4,288,128]{2,1,0:T(8,128)(2,1)S(1)}, bf16[4,288,128]{2,1,0:T(8,128)(2,1)S(1)}) custom-call(s32[1]{0:T(128)} %bitcast.6.req_ref, s32[2,32]{1,0:T(2,128)S(1)} %bitcast.9, bf16[2,288,128]{2,1,0:T(8,128)(2,1)S(1)} %pages.1.refs_0_, ...), custom_call_target="tpu_custom_call" | custom-call | tf_op jit(solution)/shard_map/relay_pages/pallas_call | solution.py:438
  114.9 0.7 collective-permute-start.18
  115.6 2.3 %collective-permute-start.19 = (bf16[4,288,128]{2,1,0:T(8,128)(2,1)S(1)}, bf16[4,288,128]{2,1,0:T(8,128)(2,1)S(1)}, u32[]{:S(2)}, u32[]{:S(2)}) collective-permute-start(bf16[4,288,128]{2,1,0:T(8,128)(2,1)S(1)} %get-tuple-element.50), channel_id=1, source_target_pairs={{0,128},{8,136},{16,144},{24,152},{32,160},{40,168},{48,176},{56,1... | collective-permute-start | bytes 884744 | tf_op jit(solution)/shard_map/ppermute | solution.py:520
  117.9 0.0 collective-permute-start.20
  117.9 4.4 %collective-permute-done.18.refs_1_ = bf16[4,288,128]{2,1,0:T(8,128)(2,1)S(1)} collective-permute-done((bf16[4,288,128]{2,1,0:T(8,128)(2,1)S(1)}, bf16[4,288,128]{2,1,0:T(8,128)(2,1)S(1)}, u32[]{:S(2)}, u32[]{:S(2)}) %collective-permute-start.18) | collective-permute-done | bytes 294944 | tf_op jit(solution)/shard_map/ppermute | solution.py:520
  122.3 2.0 %collective-permute-done.19.refs_2_ = bf16[4,288,128]{2,1,0:T(8,128)(2,1)S(1)} collective-permute-done((bf16[4,288,128]{2,1,0:T(8,128)(2,1)S(1)}, bf16[4,288,128]{2,1,0:T(8,128)(2,1)S(1)}, u32[]{:S(2)}, u32[]{:S(2)}) %collective-permute-start.19) | collective-permute-done | bytes 294944 | tf_op jit(solution)/shard_map/ppermute | solution.py:520
  124.3 3.1 %collective-permute-done.20.refs_3_ = bf16[4,288,128]{2,1,0:T(8,128)(2,1)S(1)} collective-permute-done((bf16[4,288,128]{2,1,0:T(8,128)(2,1)S(1)}, bf16[4,288,128]{2,1,0:T(8,128)(2,1)S(1)}, u32[]{:S(2)}, u32[]{:S(2)}) %collective-permute-start.20) | collective-permute-done | bytes 294944 | tf_op jit(solution)/shard_map/ppermute | solution.py:520
  127.4 0.3 shard_map.95
  127.7 0.1 collective-permute-start.21
  127.8 11.7 %attend.3 = (bf16[128,512]{1,0:T(8,128)(2,1)}, bf16[128,512]{1,0:T(8,128)(2,1)}, bf16[128,512]{1,0:T(8,128)(2,1)}, bf16[128,512]{1,0:T(8,128)(2,1)}, bf16[128,51...) custom-call(s32[1]{0:T(128)} %bitcast.refs_0_.ctx_ref, ...), custom_call_target="tpu_custom_call" | custom-call | flops 4400000000 | bytes 6000000 | tf_op jit(solution)/shard_map/attend/pallas_call | solution.py:294
  139.5 0.7 collective-permute-start.10
  140.2 3.3 %collective-permute-start.11 = (bf16[128,512]{1,0:T(8,128)(2,1)}, bf16[128,512]{1,0:T(8,128)(2,1)S(1)}, u32[]{:S(2)}, u32[]{:S(2)}) collective-permute-start(bf16[128,512]{1,0:T(8,128)(2,1)} %get-tuple-element.43), channel_id=1, source_target_pairs={{5,0},{6,1},{7,2},{4,3},{1,4},{2,5},{3,6},{0,7},{13,8},{14,9},{15,... | collective-permute-start | bytes 393224 | tf_op jit(solution)/shard_map/ppermute | solution.py:559
  143.5 0.0 collective-permute-start.12
  143.5 2.6 %collective-permute-start.13 = (bf16[128,512]{1,0:T(8,128)(2,1)}, bf16[128,512]{1,0:T(8,128)(2,1)S(1)}, u32[]{:S(2)}, u32[]{:S(2)}) collective-permute-start(bf16[128,512]{1,0:T(8,128)(2,1)} %get-tuple-element.45), channel_id=1, source_target_pairs={{2,0},{3,1},{0,2},{1,3},{6,4},{7,5},{4,6},{5,7},{10,8},{11,9},{8,1... | collective-permute-start | bytes 393224 | tf_op jit(solution)/shard_map/ppermute | solution.py:559
  146.1 0.0 collective-permute-done.21.crossed_ref
  146.1 1.4 collective-permute-start.14
  147.5 0.0 collective-permute-done.10.refs_3_
  147.5 3.7 %collective-permute-start.8 = (bf16[128,512]{1,0:T(8,128)(2,1)}, bf16[128,512]{1,0:T(8,128)(2,1)S(1)}, u32[]{:S(2)}, u32[]{:S(2)}) collective-permute-start(bf16[128,512]{1,0:T(8,128)(2,1)} %get-tuple-element.40), channel_id=1, source_target_pairs={{1,0},{2,1},{3,2},{0,3},{5,4},{6,5},{7,6},{4,7},{9,8},{10,9},{11,1... | collective-permute-start | bytes 393224 | tf_op jit(solution)/shard_map/ppermute | solution.py:559
  151.2 0.3 collective-permute-start.9
  151.4 0.3 shard_map.96
  151.7 0.7 reshape.67
  152.4 1.0 unpack.2.refs_8_
  153.5 0.3 collective-permute-done.12.refs_5_
  153.8 2.0 %collective-permute-done.13.refs_6_ = bf16[128,512]{1,0:T(8,128)(2,1)S(1)} collective-permute-done((bf16[128,512]{1,0:T(8,128)(2,1)}, bf16[128,512]{1,0:T(8,128)(2,1)S(1)}, u32[]{:S(2)}, u32[]{:S(2)}) %collective-permute-start.13) | collective-permute-done | bytes 131104 | tf_op jit(solution)/shard_map/ppermute | solution.py:559
  155.8 0.9 collective-permute-done.14.refs_7_
  156.7 0.9 collective-permute-done.8.refs_1_
  157.6 1.6 %collective-permute-done.9.refs_2_ = bf16[128,512]{1,0:T(8,128)(2,1)S(1)} collective-permute-done((bf16[128,512]{1,0:T(8,128)(2,1)}, bf16[128,512]{1,0:T(8,128)(2,1)S(1)}, u32[]{:S(2)}, u32[]{:S(2)}) %collective-permute-start.9) | collective-permute-done | bytes 131104 | tf_op jit(solution)/shard_map/ppermute | solution.py:559
  159.3 1.0 unpack.3
  (34 shorter events, 0.1 us)
Async XLA Ops:
  0.6 8.5 %copy-start.8 = (bf16[1,128,576]{1,2,0:T(8,128)(2,1)S(1)}, bf16[1,128,576]{1,2,0:T(8,128)(2,1)}, u32[]{:S(2)}) copy-start(bf16[1,128,576]{1,2,0:T(8,128)(2,1)} %param.9) | copy-start | bytes 442372
  3.0 28.9 %copy-start = (bf16[1,128,12288]{2,1,0:T(8,128)(2,1)S(1)}, bf16[1,128,12288]{2,1,0:T(8,128)(2,1)}, u32[]{:S(2)}) copy-start(bf16[1,128,12288]{2,1,0:T(8,128)(2,1)} %refs_1_.3) | copy-start | bytes 9437188
  3.0 78.6 %all-to-all-start = ((bf16[8,128,768]{2,1,0:T(8,128)(2,1)}), bf16[8,128,768]{2,1,0:T(8,128)(2,1)}, u32[]{:S(2)}, u32[]{:S(2)}) async-start(bf16[8,128,768]{2,1,0:T(8,128)(2,1)} %pack_all.1), calls=%async_computation | async-start | bytes 3145728 | tf_op jit(solution)/shard_map/all_to_all | solution.py:527
  9.3 31.2 %copy-start.1 = (bf16[128,640]{1,0:T(8,128)(2,1)}, bf16[128,640]{1,0:T(8,128)(2,1)S(1)}, u32[]{:S(2)}) copy-start(bf16[128,640]{1,0:T(8,128)(2,1)S(1)} %pad.4.refs_2_.refs_15_.kv_ref) | copy-start | bytes 491524
  9.3 22.6 %collective-permute-start = (bf16[128,640]{1,0:T(8,128)(2,1)S(1)}, bf16[128,640]{1,0:T(8,128)(2,1)S(1)}, u32[]{:S(2)}, u32[]{:S(2)}) collective-permute-start(bf16[128,640]{1,0:T(8,128)(2,1)S(1)} %pad.4.refs_2_.refs_15_.kv_ref), channel_id=1, source_target_pairs={{0,4},{1,5},{2,6},{3,7},{4,0},{5,1},{6,2},{7,3},{8,12},{9,13},{10,... | collective-permute-start | bytes 491528 | tf_op jit(solution)/shard_map/ppermute | solution.py:535
  31.9 8.6 %copy-start.3 = (bf16[128,640]{1,0:T(8,128)(2,1)}, bf16[128,640]{1,0:T(8,128)(2,1)S(1)}, u32[]{:S(2)}) copy-start(bf16[128,640]{1,0:T(8,128)(2,1)S(1)} %collective-permute-done.refs_3_.refs_16_) | copy-start | bytes 491524
  33.2 27.9 %collective-permute-start.1 = (bf16[128,2048]{1,0:T(8,128)(2,1)}, bf16[128,2048]{1,0:T(8,128)(2,1)S(1)}, u32[]{:S(2)}, u32[]{:S(2)}) collective-permute-start(bf16[128,2048]{1,0:T(8,128)(2,1)} %get-tuple-element.27), channel_id=1, source_target_pairs={{0,1},{1,2},{2,3},{3,0},{4,5},{5,6},{6,7},{7,4},{8,9},{9,10},{10,1... | collective-permute-start | bytes 1572872 | tf_op jit(solution)/shard_map/ppermute | solution.py:541
  34.7 31.7 %collective-permute-start.2 = (bf16[128,2048]{1,0:T(8,128)(2,1)}, bf16[128,2048]{1,0:T(8,128)(2,1)S(1)}, u32[]{:S(2)}, u32[]{:S(2)}) collective-permute-start(bf16[128,2048]{1,0:T(8,128)(2,1)} %get-tuple-element.30), channel_id=1, source_target_pairs={{0,3},{1,0},{2,1},{3,2},{4,7},{5,4},{6,5},{7,6},{8,11},{9,8},{10,9... | collective-permute-start | bytes 1572872 | tf_op jit(solution)/shard_map/ppermute | solution.py:541
  36.5 31.6 %collective-permute-start.6 = (bf16[128,2048]{1,0:T(8,128)(2,1)S(1)}, bf16[128,2048]{1,0:T(8,128)(2,1)S(1)}, u32[]{:S(2)}, u32[]{:S(2)}) collective-permute-start(bf16[128,2048]{1,0:T(8,128)(2,1)S(1)} %get-tuple-element.34), channel_id=1, source_target_pairs={{0,2},{1,3},{2,0},{3,1},{4,6},{5,7},{6,4},{7,5},{8,10},{9,11},{10,... | collective-permute-start | bytes 1572872 | tf_op jit(solution)/shard_map/ppermute | solution.py:541
  40.5 7.9 %collective-permute-start.3 = (bf16[128,768]{1,0:T(8,128)(2,1)}, bf16[128,768]{1,0:T(8,128)(2,1)S(1)}, u32[]{:S(2)}, u32[]{:S(2)}) collective-permute-start(bf16[128,768]{1,0:T(8,128)(2,1)} %get-tuple-element.31), channel_id=1, source_target_pairs={{0,4},{1,5},{2,6},{3,7},{4,0},{5,1},{6,2},{7,3},{8,12},{9,13},{10,... | collective-permute-start | bytes 589832 | tf_op jit(solution)/shard_map/ppermute | solution.py:541
  41.1 11.6 %collective-permute-start.4 = (bf16[128,768]{1,0:T(8,128)(2,1)}, bf16[128,768]{1,0:T(8,128)(2,1)S(1)}, u32[]{:S(2)}, u32[]{:S(2)}) collective-permute-start(bf16[128,768]{1,0:T(8,128)(2,1)} %get-tuple-element.32), channel_id=1, source_target_pairs={{0,5},{1,6},{2,7},{3,4},{4,1},{5,2},{6,3},{7,0},{8,13},{9,14},{10,... | collective-permute-start | bytes 589832 | tf_op jit(solution)/shard_map/ppermute | solution.py:541
  48.3 19.8 %copy-start.12 = (bf16[128,768]{1,0:T(8,128)(2,1)}, bf16[128,768]{1,0:T(8,128)(2,1)S(1)}, u32[]{:S(2)}) copy-start(bf16[128,768]{1,0:T(8,128)(2,1)S(1)} %collective-permute-done.3.refs_6_) | copy-start | bytes 589828
  48.3 9.6 %collective-permute-start.5 = (bf16[128,768]{1,0:T(8,128)(2,1)}, bf16[128,768]{1,0:T(8,128)(2,1)S(1)}, u32[]{:S(2)}, u32[]{:S(2)}) collective-permute-start(bf16[128,768]{1,0:T(8,128)(2,1)} %get-tuple-element.33), channel_id=1, source_target_pairs={{0,7},{1,4},{2,5},{3,6},{4,3},{5,0},{6,1},{7,2},{8,15},{9,12},{10,... | collective-permute-start | bytes 589832 | tf_op jit(solution)/shard_map/ppermute | solution.py:541
  52.7 15.4 %copy-start.13 = (bf16[128,768]{1,0:T(8,128)(2,1)}, bf16[128,768]{1,0:T(8,128)(2,1)S(1)}, u32[]{:S(2)}) copy-start(bf16[128,768]{1,0:T(8,128)(2,1)S(1)} %collective-permute-done.4.refs_7_) | copy-start | bytes 589828
  52.7 8.4 %collective-permute-start.7 = (bf16[128,768]{1,0:T(8,128)(2,1)}, bf16[128,768]{1,0:T(8,128)(2,1)S(1)}, u32[]{:S(2)}, u32[]{:S(2)}) collective-permute-start(bf16[128,768]{1,0:T(8,128)(2,1)} %get-tuple-element.35), channel_id=1, source_target_pairs={{0,6},{1,7},{2,4},{3,5},{4,2},{5,3},{6,0},{7,1},{8,14},{9,15},{10,... | collective-permute-start | bytes 589832 | tf_op jit(solution)/shard_map/ppermute | solution.py:541
  58.0 10.2 %copy-start.14 = (bf16[128,768]{1,0:T(8,128)(2,1)}, bf16[128,768]{1,0:T(8,128)(2,1)S(1)}, u32[]{:S(2)}) copy-start(bf16[128,768]{1,0:T(8,128)(2,1)S(1)} %collective-permute-done.5.refs_8_) | copy-start | bytes 589828
  61.1 7.1 %copy-start.15 = (bf16[128,768]{1,0:T(8,128)(2,1)}, bf16[128,768]{1,0:T(8,128)(2,1)S(1)}, u32[]{:S(2)}) copy-start(bf16[128,768]{1,0:T(8,128)(2,1)S(1)} %collective-permute-done.7.refs_10_) | copy-start | bytes 589828
  61.1 7.1 %copy-start.9 = (bf16[128,2048]{1,0:T(8,128)(2,1)}, bf16[128,2048]{1,0:T(8,128)(2,1)S(1)}, u32[]{:S(2)}) copy-start(bf16[128,2048]{1,0:T(8,128)(2,1)S(1)} %collective-permute-done.1.refs_4_) | copy-start | bytes 1572868
  66.5 1.7 %copy-start.10 = (bf16[128,2048]{1,0:T(8,128)(2,1)}, bf16[128,2048]{1,0:T(8,128)(2,1)S(1)}, u32[]{:S(2)}) copy-start(bf16[128,2048]{1,0:T(8,128)(2,1)S(1)} %collective-permute-done.2.refs_5_) | copy-start | bytes 1572868
  68.1 0.8 copy-start.11
  81.5 3.8 %copy-start.2 = (bf16[128,640]{1,0:T(8,128)(2,1)S(1)}, bf16[128,640]{1,0:T(8,128)(2,1)}, u32[]{:S(2)}) copy-start(bf16[128,640]{1,0:T(8,128)(2,1)} %copy-done.1) | copy-start | bytes 491524
  81.5 3.8 %copy-start.6 = (f32[512]{0:T(512)S(1)}, f32[512]{0:T(512)}, u32[]{:S(2)}) copy-start(f32[512]{0:T(512)} %param.10) | copy-start | bytes 6148
  81.5 3.8 %copy-start.7 = (s32[1,16]{1,0:T(1,128)S(1)}, s32[1,16]{1,0:T(1,128)}, u32[]{:S(2)}) copy-start(s32[1,16]{1,0:T(1,128)} %param.14) | copy-start | bytes 196
  81.6 31.1 %copy-start.5 = (s32[32,2]{0,1:T(2,128)S(1)}, s32[32,2]{0,1:T(2,128)}, u32[]{:S(2)}) copy-start(s32[32,2]{0,1:T(2,128)} %param.15) | copy-start | bytes 772
  81.6 70.9 %all-to-all-start.1 = ((bf16[8,128,512]{2,1,0:T(8,128)(2,1)}), bf16[8,128,512]{2,1,0:T(8,128)(2,1)S(1)}, u32[]{:S(2)}, u32[]{:S(2)}) async-start(bf16[8,128,512]{2,1,0:T(8,128)(2,1)} %bitcast.17), calls=%async_computation.1 | async-start | bytes 2097152 | tf_op jit(solution)/shard_map/all_to_all | solution.py:527
  86.3 19.8 %collective-permute-start.15 = (bf16[2,288,128]{2,1,0:T(8,128)(2,1)S(1)}, bf16[2,288,128]{2,1,0:T(8,128)(2,1)S(1)}, u32[]{:S(2)}, u32[]{:S(2)}) collective-permute-start(bf16[2,288,128]{2,1,0:T(8,128)(2,1)S(1)} %pages.1.refs_0_), channel_id=1, source_target_pairs={{0,16},{8,24},{16,32},{24,40},{32,48},{40,56},{48,0},{56,8},{64,80... | collective-permute-start | bytes 442376 | tf_op jit(solution)/shard_map/ppermute | solution.py:518
  90.0 22.6 %collective-permute-start.16 = (bf16[2,288,128]{2,1,0:T(8,128)(2,1)S(1)}, bf16[2,288,128]{2,1,0:T(8,128)(2,1)S(1)}, u32[]{:S(2)}, u32[]{:S(2)}) collective-permute-start(bf16[2,288,128]{2,1,0:T(8,128)(2,1)S(1)} %pages.1.refs_0_), channel_id=1, source_target_pairs={{0,32},{8,40},{16,48},{24,56},{32,0},{40,8},{48,16},{56,24},{64,96... | collective-permute-start | bytes 442376 | tf_op jit(solution)/shard_map/ppermute | solution.py:518
  91.0 21.6 %collective-permute-start.17 = (bf16[2,288,128]{2,1,0:T(8,128)(2,1)S(1)}, bf16[2,288,128]{2,1,0:T(8,128)(2,1)S(1)}, u32[]{:S(2)}, u32[]{:S(2)}) collective-permute-start(bf16[2,288,128]{2,1,0:T(8,128)(2,1)S(1)} %pages.1.refs_0_), channel_id=1, source_target_pairs={{0,48},{8,56},{16,0},{24,8},{32,16},{40,24},{48,32},{56,40},{64,11... | collective-permute-start | bytes 442376 | tf_op jit(solution)/shard_map/ppermute | solution.py:518
  114.9 7.4 %collective-permute-start.18 = (bf16[4,288,128]{2,1,0:T(8,128)(2,1)S(1)}, bf16[4,288,128]{2,1,0:T(8,128)(2,1)S(1)}, u32[]{:S(2)}, u32[]{:S(2)}) collective-permute-start(bf16[4,288,128]{2,1,0:T(8,128)(2,1)S(1)} %get-tuple-element.49), channel_id=1, source_target_pairs={{0,64},{8,72},{16,80},{24,88},{32,96},{40,104},{48,112},{56,120},{... | collective-permute-start | bytes 884744 | tf_op jit(solution)/shard_map/ppermute | solution.py:520
  115.6 8.7 %collective-permute-start.19 = (bf16[4,288,128]{2,1,0:T(8,128)(2,1)S(1)}, bf16[4,288,128]{2,1,0:T(8,128)(2,1)S(1)}, u32[]{:S(2)}, u32[]{:S(2)}) collective-permute-start(bf16[4,288,128]{2,1,0:T(8,128)(2,1)S(1)} %get-tuple-element.50), channel_id=1, source_target_pairs={{0,128},{8,136},{16,144},{24,152},{32,160},{40,168},{48,176},{56,1... | collective-permute-start | bytes 884744 | tf_op jit(solution)/shard_map/ppermute | solution.py:520
  117.9 9.5 %collective-permute-start.20 = (bf16[4,288,128]{2,1,0:T(8,128)(2,1)S(1)}, bf16[4,288,128]{2,1,0:T(8,128)(2,1)S(1)}, u32[]{:S(2)}, u32[]{:S(2)}) collective-permute-start(bf16[4,288,128]{2,1,0:T(8,128)(2,1)S(1)} %get-tuple-element.51), channel_id=1, source_target_pairs={{0,192},{8,200},{16,208},{24,216},{32,224},{40,232},{48,240},{56,2... | collective-permute-start | bytes 884744 | tf_op jit(solution)/shard_map/ppermute | solution.py:520
  127.7 18.4 %collective-permute-start.21 = (bf16[2,288,128]{2,1,0:T(8,128)(2,1)S(1)}, bf16[2,288,128]{2,1,0:T(8,128)(2,1)S(1)}, u32[]{:S(2)}, u32[]{:S(2)}) collective-permute-start(bf16[2,288,128]{2,1,0:T(8,128)(2,1)S(1)} %shard_map.95), channel_id=1, source_target_pairs={{0,8},{8,0},{16,24},{24,16},{32,40},{40,32},{48,56},{56,48},{64,72... | collective-permute-start | bytes 442376 | tf_op jit(solution)/shard_map/ppermute | solution.py:522
  139.5 8.0 %collective-permute-start.10 = (bf16[128,512]{1,0:T(8,128)(2,1)}, bf16[128,512]{1,0:T(8,128)(2,1)S(1)}, u32[]{:S(2)}, u32[]{:S(2)}) collective-permute-start(bf16[128,512]{1,0:T(8,128)(2,1)} %get-tuple-element.42), channel_id=1, source_target_pairs={{4,0},{5,1},{6,2},{7,3},{0,4},{1,5},{2,6},{3,7},{12,8},{13,9},{14,... | collective-permute-start | bytes 393224 | tf_op jit(solution)/shard_map/ppermute | solution.py:559
  140.2 11.0 %collective-permute-start.11 = (bf16[128,512]{1,0:T(8,128)(2,1)}, bf16[128,512]{1,0:T(8,128)(2,1)S(1)}, u32[]{:S(2)}, u32[]{:S(2)}) collective-permute-start(bf16[128,512]{1,0:T(8,128)(2,1)} %get-tuple-element.43), channel_id=1, source_target_pairs={{5,0},{6,1},{7,2},{4,3},{1,4},{2,5},{3,6},{0,7},{13,8},{14,9},{15,... | collective-permute-start | bytes 393224 | tf_op jit(solution)/shard_map/ppermute | solution.py:559
  143.5 10.3 %collective-permute-start.12 = (bf16[128,512]{1,0:T(8,128)(2,1)}, bf16[128,512]{1,0:T(8,128)(2,1)S(1)}, u32[]{:S(2)}, u32[]{:S(2)}) collective-permute-start(bf16[128,512]{1,0:T(8,128)(2,1)} %get-tuple-element.44), channel_id=1, source_target_pairs={{7,0},{4,1},{5,2},{6,3},{3,4},{0,5},{1,6},{2,7},{15,8},{12,9},{13,... | collective-permute-start | bytes 393224 | tf_op jit(solution)/shard_map/ppermute | solution.py:559
  143.5 12.3 %collective-permute-start.13 = (bf16[128,512]{1,0:T(8,128)(2,1)}, bf16[128,512]{1,0:T(8,128)(2,1)S(1)}, u32[]{:S(2)}, u32[]{:S(2)}) collective-permute-start(bf16[128,512]{1,0:T(8,128)(2,1)} %get-tuple-element.45), channel_id=1, source_target_pairs={{2,0},{3,1},{0,2},{1,3},{6,4},{7,5},{4,6},{5,7},{10,8},{11,9},{8,1... | collective-permute-start | bytes 393224 | tf_op jit(solution)/shard_map/ppermute | solution.py:559
  146.1 10.6 %collective-permute-start.14 = (bf16[128,512]{1,0:T(8,128)(2,1)}, bf16[128,512]{1,0:T(8,128)(2,1)S(1)}, u32[]{:S(2)}, u32[]{:S(2)}) collective-permute-start(bf16[128,512]{1,0:T(8,128)(2,1)} %get-tuple-element.46), channel_id=1, source_target_pairs={{6,0},{7,1},{4,2},{5,3},{2,4},{3,5},{0,6},{1,7},{14,8},{15,9},{12,... | collective-permute-start | bytes 393224 | tf_op jit(solution)/shard_map/ppermute | solution.py:559
  147.5 10.1 %collective-permute-start.8 = (bf16[128,512]{1,0:T(8,128)(2,1)}, bf16[128,512]{1,0:T(8,128)(2,1)S(1)}, u32[]{:S(2)}, u32[]{:S(2)}) collective-permute-start(bf16[128,512]{1,0:T(8,128)(2,1)} %get-tuple-element.40), channel_id=1, source_target_pairs={{1,0},{2,1},{3,2},{0,3},{5,4},{6,5},{7,6},{4,7},{9,8},{10,9},{11,1... | collective-permute-start | bytes 393224 | tf_op jit(solution)/shard_map/ppermute | solution.py:559
  151.2 8.1 %copy-start.4 = (bf16[128,512]{1,0:T(8,128)(2,1)S(1)}, bf16[128,512]{1,0:T(8,128)(2,1)}, u32[]{:S(2)}) copy-start(bf16[128,512]{1,0:T(8,128)(2,1)} %get-tuple-element.39.refs_0_) | copy-start | bytes 393220
  151.2 8.1 %collective-permute-start.9 = (bf16[128,512]{1,0:T(8,128)(2,1)}, bf16[128,512]{1,0:T(8,128)(2,1)S(1)}, u32[]{:S(2)}, u32[]{:S(2)}) collective-permute-start(bf16[128,512]{1,0:T(8,128)(2,1)} %get-tuple-element.41), channel_id=1, source_target_pairs={{3,0},{0,1},{1,2},{2,3},{7,4},{4,5},{5,6},{6,7},{11,8},{8,9},{9,10... | collective-permute-start | bytes 393224 | tf_op jit(solution)/shard_map/ppermute | solution.py:559
